TPU v7x, 32 devices: a whole 2x2x4 slice. The times are simulated.
32 devices in a mesh: grp: 2 (over y), exp: 4 (over x, core), hid: 4 (over z).
Axes of the slice: x: 2, y: 2, z: 4, core: 2. Of those that a mesh axis runs over, the one named last changes fastest.
Arguments:
- tokens: bfloat16 [1024, 4096], P(('grp', 'exp'), 'hid'), parts along dimension 0, may hold values from -6 to 6
- grad_out: bfloat16 [1024, 4096], P(('grp', 'exp'), 'hid'), parts along dimension 0, may hold values from -3 to 3
- gates: bfloat16 [1024, 2], P(('grp', 'exp')), parts along dimension 0, may hold values from 0.049804688 to 1
- block_experts: int32 [8, 2], P('grp'), parts along dimension 0, may hold values from 0 to 3, all different within a row; in each aligned block of 4 rows (0 to 3, 4 to 7, ...) at most 2 rows name the same one
- w_gate: bfloat16 [4, 4096, 8192], P('exp', None, 'hid'), may hold values from -0.125 to 0.125
- w_up: bfloat16 [4, 4096, 8192], P('exp', None, 'hid'), may hold values from -0.125 to 0.125
- w_down: bfloat16 [4, 8192, 4096], P('exp', 'hid'), may hold values from -0.0625 to 0.0625
Outputs:
- d_tokens: bfloat16 [1024, 4096], P(('grp', 'exp'), 'hid'), parts along dimension 0
- d_gates: float32 [1024, 2], P(('grp', 'exp')), parts along dimension 0
There are 2 independent parts, one for each index of `grp`. A program takes and returns all parts, laid end to end along the dimension named above; an argument that names none is the same for every part. Nothing has to cross between parts.
Inputs may be any that keep to these rules, and one draw needn't show every extreme that they name: `block_experts`: each row names two different experts for one block of 128 tokens; no expert is named by more than 2 of the 4 blocks, one expert by exactly 2, and every expert by some block.
All inputs are finite; a program needn't handle non-finite values.
Results may differ from a plain program's by a relative error of at most 0.0049.
Values may be sent and summed in bfloat16 or wider, within the bound.
A program may use at most 192 MiB of HBM per device.

v0:
```python
import jax
import jax.numpy as jnp
from jax import lax
from jax.sharding import PartitionSpec as P

BLOCK = 128


HIGHEST = lax.Precision.HIGHEST
CONTRACT_LAST = (((1,), (1,)), ((), ()))


def passed_along(block, axis, distance):
    devices = range(lax.axis_size(axis))
    route = [((i - distance) % len(devices), i) for i in devices]
    return lax.ppermute(block, axis, route)


def local(tokens, grad_out, gates, block_experts, w_gate, w_up, w_down):
    n_experts = lax.axis_size("exp")
    own_index = lax.axis_index("exp")
    tok_dev, width_dev = tokens.shape
    blocks_all = block_experts.shape[0]
    per_home = tok_dev // BLOCK
    capacity = blocks_all // 2
    used_count = capacity * BLOCK
    w_one = w_gate[0]
    w_three = w_up[0]
    w_two = w_down[0]
    matched = block_experts == own_index
    chosen = jnp.any(matched, axis=1)
    slot_of = matched[:, 1].astype(jnp.int32)
    position = jnp.cumsum(chosen.astype(jnp.int32)) - 1
    placed = (position[None, :] == jnp.arange(capacity, dtype=jnp.int32)[:, None]) & chosen[None, :]
    placed_int = placed.astype(jnp.int32)
    list_block = jnp.sum(placed_int * jnp.arange(blocks_all, dtype=jnp.int32)[None, :], axis=1)
    list_slot = jnp.sum(placed_int * slot_of[None, :], axis=1)
    live = jnp.any(placed, axis=1)
    row_index = (list_block[:, None] * BLOCK + jnp.arange(BLOCK, dtype=jnp.int32)[None, :]).reshape(
        used_count
    )
    x_home, dy_home, gate_home = (
        lax.all_gather(tokens, "exp", axis=0, tiled=True),
        lax.all_gather(grad_out, "exp", axis=0, tiled=True),
        lax.all_gather(gates, "exp", axis=0, tiled=True),
    )
    gate_pick = (
        jnp.take(gate_home, row_index, axis=0).astype(jnp.float32).reshape(capacity, BLOCK, 2)
    )
    slot_hot = (list_slot[:, None] == jnp.arange(2, dtype=jnp.int32)[None, :]).astype(jnp.float32)
    slot_hot = slot_hot * live[:, None].astype(jnp.float32)
    gate_column = jnp.sum(gate_pick * slot_hot[:, None, :], axis=2).reshape(used_count)
    x_piece = jnp.take(lax.all_gather(x_home, "hid", axis=1, tiled=True), row_index, axis=0)
    dy_piece = jnp.take(lax.all_gather(dy_home, "hid", axis=1, tiled=True), row_index, axis=0)
    one_rows = w_one
    three_rows = w_three
    pre_gate = jnp.dot(x_piece, one_rows, preferred_element_type=jnp.float32)
    pre_up = jnp.dot(x_piece, three_rows, preferred_element_type=jnp.float32)
    d_hidden = lax.dot_general(dy_piece, w_two, CONTRACT_LAST, preferred_element_type=jnp.float32)
    sigmoid_gate = jax.nn.sigmoid(pre_gate)
    activated = pre_gate * sigmoid_gate
    score_part = jnp.sum(activated * pre_up * d_hidden, axis=1)
    score = lax.psum(score_part, "hid")
    scaled = gate_column[:, None] * d_hidden
    d_pre_gate = (scaled * pre_up * sigmoid_gate * (1.0 + pre_gate * (1.0 - sigmoid_gate))).astype(
        jnp.bfloat16
    )
    d_pre_up = (scaled * activated).astype(jnp.bfloat16)
    one_rows = w_one
    three_rows = w_three
    first = lax.dot_general(one_rows, d_pre_gate, CONTRACT_LAST, preferred_element_type=jnp.float32)
    owned = lax.psum_scatter(
        first
        + lax.dot_general(three_rows, d_pre_up, CONTRACT_LAST, preferred_element_type=jnp.float32),
        "hid",
        scatter_dimension=0,
        tiled=True,
    )
    result_cols = owned.reshape(width_dev, capacity, BLOCK)
    score_blocks = score.reshape(capacity, BLOCK)

    def share(home):
        wanted = home * per_home + jnp.arange(per_home, dtype=jnp.int32)
        select = ((list_block[None, :] == wanted[:, None]) & live[None, :]).astype(jnp.float32)
        grad_part = jnp.einsum("bi,dir->dbr", select, result_cols, precision=HIGHEST).reshape(
            width_dev, tok_dev
        )
        gate_part = jnp.einsum(
            "bi,ik,ir->kbr", select, slot_hot, score_blocks, precision=HIGHEST
        ).reshape(2, tok_dev)
        return (grad_part, gate_part)

    zero_totals = (
        jnp.zeros((width_dev, tok_dev), jnp.float32),
        jnp.zeros((2, tok_dev), jnp.float32),
    )

    def single_turn(step, totals):
        grad_part, gate_part = share((own_index + 1 + step) % n_experts)
        return passed_along((totals[0] + grad_part, totals[1] + gate_part), "exp", -1)

    totals = lax.fori_loop(0, n_experts - 1, single_turn, zero_totals)
    grad_part, gate_part = share(own_index)
    grad_total = totals[0] + grad_part
    gate_total = totals[1] + gate_part
    d_tokens = grad_total.T.astype(jnp.bfloat16)
    d_gates = gate_total.T
    return (d_tokens, d_gates)


def solution(mesh):
    placed = (
        P(("grp", "exp"), "hid"),
        P(("grp", "exp"), "hid"),
        P(("grp", "exp"), None),
        P("grp", None),
        P("exp", None, "hid"),
        P("exp", None, "hid"),
        P("exp", "hid", None),
    )
    return jax.shard_map(
        local,
        mesh=mesh,
        in_specs=placed,
        out_specs=(P(("grp", "exp"), "hid"), P(("grp", "exp"), None)),
        check_vma=False,
    )
```

profile of v0, /device:TPU:11, one launch (start us, length us, event | category | flops | bytes accessed | tf_op | source)
XLA Modules:
  0.0 381.8 jit_solution(17595849389789333251)
XLA Ops:
  7.2 0.7 all-gather.9.cloned.1.call-update
  8.0 0.7 all-gather.5.cloned.1.call-update
  8.7 18.2 %all-gather.9.cloned.1.call-done = bf16[512,1024]{1,0:T(8,128)(2,1)} async-done(((bf16[128,1024]{1,0:T(8,128)(2,1)}), bf16[512,1024]{1,0:T(8,128)(2,1)}) %all-gather.9.cloned.1.call-update) | async-done | bytes 1048592 | tf_op jit(solution)/shard_map/all_gather | solution.py:43
  27.0 18.2 %all-gather.5.cloned.1.call-done = bf16[512,1024]{1,0:T(8,128)(2,1)} async-done(((bf16[128,1024]{1,0:T(8,128)(2,1)}), bf16[512,1024]{1,0:T(8,128)(2,1)}) %all-gather.5.cloned.1.call-update) | async-done | bytes 1048592 | tf_op jit(solution)/shard_map/all_gather | solution.py:44
  45.4 0.1 copy.12
  45.5 0.2 reduce-window.8
  45.7 5.5 %all_gather.15 = bf16[512,2]{1,0:T(8,128)(2,1)S(1)} all-gather(bf16[128,2]{1,0:T(8,128)(2,1)S(1)} %copy.12), channel_id=1, replica_groups=mesh['grp'=2,'exp'=4,'hid'=4] {'exp'}, dimensions={0}, use_global_device_ids=true | all-gather | bytes 2560 | tf_op jit(solution)/shard_map/all_gather | solution.py:45
  51.2 0.1 fusion.53
  51.4 0.1 select_reduce_fusion
  51.5 0.1 iota_add_fusion
  51.6 0.9 gather_fusion
  52.5 0.1 and_bitcast_fusion
  52.6 0.1 compare_select_fusion.4
  52.6 0.2 fusion.41
  52.8 0.1 compare_and_fusion.2
  52.9 72.8 %all-gather.11.cloned.1.call-done = bf16[512,4096]{1,0:T(8,128)(2,1)} async-done(((bf16[512,1024]{1,0:T(8,128)(2,1)}), bf16[512,4096]{1,0:T(8,128)(2,1)}) %all-gather.11.cloned.1.call-update) | async-done | bytes 4194320 | tf_op jit(solution)/shard_map/all_gather | solution.py:53
  125.7 6.6 %gather_fusion.2 = bf16[256,4096]{1,0:T(8,128)(2,1)S(1)} fusion(bf16[512,4096]{1,0:T(8,128)(2,1)} %all-gather.11.cloned.1.call-done, s32[1024]{0:T(1024)S(1)} %pad_clamp_fusion), kind=kCustom, calls=%fused_computation.1.clone | custom fusion | bytes 4195328 | tf_op jit(solution)/shard_map/jit(_take)/gather | solution.py:53
  132.3 10.6 %fusion.16 = f32[256,2048]{1,0:T(8,128)} fusion(bf16[1,4096,2048]{2,1,0:T(8,128)(2,1)} %param.15, bf16[256,4096]{1,0:T(8,128)(2,1)S(1)} %gather_fusion.2, pred[256]{0:T(512)(128)(4,1)S(1)} %get-tuple-element.295), kind=kOutput, calls=%fused_computation.20 | convolution fusion | flops 4296015872 | bytes 20971776 | tf_op jit(solution)/shard_map/dot_general | solution.py:57
  142.9 9.7 %fusion.20 = f32[256,2048]{1,0:T(8,128)} fusion(bf16[1,4096,2048]{2,1,0:T(8,128)(2,1)} %param.16, bf16[256,4096]{1,0:T(8,128)(2,1)S(1)} %gather_fusion.2, pred[256]{0:T(512)(128)(4,1)S(1)} %get-tuple-element.295), kind=kOutput, calls=%fused_computation.24 | convolution fusion | flops 4296015872 | bytes 20971776 | tf_op jit(solution)/shard_map/dot_general | solution.py:58
  152.6 53.9 %all-gather.7.cloned.1.call-done = bf16[512,4096]{1,0:T(8,128)(2,1)} async-done(((bf16[512,1024]{1,0:T(8,128)(2,1)}), bf16[512,4096]{1,0:T(8,128)(2,1)}) %all-gather.7.cloned.1.call-update) | async-done | bytes 4194320 | tf_op jit(solution)/shard_map/all_gather | solution.py:54
  206.5 6.6 %gather_fusion.1 = bf16[256,4096]{1,0:T(8,128)(2,1)S(1)} fusion(bf16[512,4096]{1,0:T(8,128)(2,1)} %all-gather.7.cloned.1.call-done, s32[1024]{0:T(1024)S(1)} %pad_clamp_fusion), kind=kCustom, calls=%fused_computation.clone | custom fusion | bytes 4195328 | tf_op jit(solution)/shard_map/jit(_take)/gather | solution.py:54
  213.1 19.0 %multiply_reduce_fusion = (f32[256]{0:T(256)S(1)}, f32[256,2048]{1,0:T(8,128)}) fusion(f32[256,2048]{1,0:T(8,128)} %fusion.20, f32[256,2048]{1,0:T(8,128)} %fusion.16, bf16[1,2048,4096]{2,1,0:T(8,128)(2,1)} %param.17, bf16[256,4096]{1,0:T(8,128)(2,1)S(1)} %gather_fusion.1, pred[256]{0:T(512)(128)(4,1)S(1)} %get-tuple-element.295), kind=kOutput, calls=%fused_computation.31 | convolution fusion | flops 4299685888 | bytes 25167104 | tf_op jit(solution)/shard_map/dot_general | solution.py:59
  232.1 14.9 %fusion.14 = f32[256,4096]{1,0:T(8,128)} fusion(bf16[1,4096,2048]{2,1,0:T(8,128)(2,1)} %param.15, f32[256,2048]{1,0:T(8,128)} %fusion.16, f32[256,2048]{1,0:T(8,128)} %fusion.20, f32[256,2048]{1,0:T(8,128)} %get-tuple-element.304, f32[256]{0:T(256)S(1)} %fusion.41), kind=kOutput, calls=%fused_computation.18 | convolution fusion | flops 4300734464 | bytes 27264000 | tf_op jit(solution)/shard_map/dot_general | solution.py:71
  247.0 11.6 %fusion.27 = f32[4096,256]{0,1:T(8,128)} fusion(f32[256,4096]{1,0:T(8,128)} %fusion.14, bf16[1,4096,2048]{2,1,0:T(8,128)(2,1)} %param.16, f32[256,2048]{1,0:T(8,128)} %get-tuple-element.304, f32[256]{0:T(256)S(1)} %fusion.41, f32[256,2048]{1,0:T(8,128)S(1)} %copy-done.2), kind=kOutput, calls=%fused_computation.29 | convolution fusion | flops 4299685888 | bytes 29361152 | tf_op jit(solution)/shard_map/dot_general | solution.py:74
  258.6 9.7 %psum.7 = f32[2,128]{1,0:T(2,128)S(1)} all-reduce(f32[2,128]{1,0:T(2,128)S(1)} %bitcast.78), channel_id=1, replica_groups=mesh['grp'=2,'exp'=4,'hid'=4] {'hid'}, use_global_device_ids=true, to_apply=%region_8.10 | all-reduce | flops 256 | bytes 2048 | tf_op jit(solution)/shard_map/psum | solution.py:63
  268.3 68.3 %reduce-scatter.2.cloned.1.call-done = f32[1024,256]{0,1:T(8,128)} async-done(((f32[4096,256]{0,1:T(8,128)}), f32[1024,256]{0,1:T(8,128)}) %reduce-scatter.2.cloned.1.call-update) | async-done | bytes 1048592 | tf_op jit(solution)/shard_map/reduce_scatter | solution.py:72
  336.6 1.5 copy.13
  338.1 2.2 fusion.42
  340.4 0.3 copy.15
  340.8 32.7 %while.18 = (s32[]{:T(128)}, f32[1024,128]{1,0:T(8,128)S(1)}, f32[2,128]{1,0:T(2,128)S(1)}, s32[]{:T(128)}, s32[2]{0:T(128)S(1)}, /*index=5*/pred[2]{0:T(512)(12...) while((s32[]{:T(128)}, f32[1024,128]{1,0:T(8,128)S(1)}, ...), condition=%wide.region_10.12_spmd.clone, body=%wide.region_9.11_spmd.clone.sunk | while | flops 3283236 | bytes 5250442 | solution.py:102
  340.8 2.1 fusion.68
  343.0 0.7 collective-permute-start
  343.7 0.3 convolution_add_fusion.3
  343.9 0.1 collective-permute-start.1
  344.0 7.7 %collective-permute-done.1 = f32[2,128]{1,0:T(2,128)S(1)} collective-permute-done((f32[2,128]{1,0:T(2,128)S(1)}, f32[2,128]{1,0:T(2,128)S(1)}, u32[]{:S(2)}, u32[]{:S(2)}) %collective-permute-start.1) | collective-permute-done | bytes 1056 | tf_op jit(solution)/shard_map/while/body/eval_jaxpr/ppermute | solution.py:16
  351.7 2.1 fusion.68
  353.9 0.1 collective-permute-start
  353.9 0.3 convolution_add_fusion.3
  354.2 0.7 collective-permute-start.1
  354.9 7.7 %collective-permute-done.1 = f32[2,128]{1,0:T(2,128)S(1)} collective-permute-done((f32[2,128]{1,0:T(2,128)S(1)}, f32[2,128]{1,0:T(2,128)S(1)}, u32[]{:S(2)}, u32[]{:S(2)}) %collective-permute-start.1) | collective-permute-done | bytes 1056 | tf_op jit(solution)/shard_map/while/body/eval_jaxpr/ppermute | solution.py:16
  362.6 2.1 fusion.68
  364.7 0.1 collective-permute-start
  364.8 0.3 convolution_add_fusion.3
  365.1 0.7 collective-permute-start.1
  365.7 7.7 %collective-permute-done.1 = f32[2,128]{1,0:T(2,128)S(1)} collective-permute-done((f32[2,128]{1,0:T(2,128)S(1)}, f32[2,128]{1,0:T(2,128)S(1)}, u32[]{:S(2)}, u32[]{:S(2)}) %collective-permute-start.1) | collective-permute-done | bytes 1056 | tf_op jit(solution)/shard_map/while/body/eval_jaxpr/ppermute | solution.py:16
  373.4 0.2 copy.14
  373.7 0.8 fusion.33
  374.5 0.8 fusion.40
  (34 shorter events, 0.6 us)
Async XLA Ops:
  7.2 38.2 %copy-start.1 = (bf16[128,2]{0,1:T(2,128)(2,1)S(1)}, bf16[128,2]{0,1:T(2,128)(2,1)}, u32[]{:S(2)}) copy-start(bf16[128,2]{0,1:T(2,128)(2,1)} %param.13) | copy-start | bytes 1540
  7.2 38.3 %copy-start = (s32[4,2]{0,1:T(2,128)S(1)}, s32[4,2]{0,1:T(2,128)}, u32[]{:S(2)}) copy-start(s32[4,2]{0,1:T(2,128)} %param.14) | copy-start | bytes 100
  7.2 19.8 %all-gather.9.cloned.1.call-start = ((), (), s32[]{:S(2)}) async-start(), calls=%async_computation.3 | async-start | bytes 1310720 | tf_op jit(solution)/shard_map/all_gather | solution.py:43
  7.9 37.4 %all-gather.5.cloned.1.call-start = ((), (), s32[]{:S(2)}) async-start(), calls=%async_computation.1 | async-start | bytes 1310720 | tf_op jit(solution)/shard_map/all_gather | solution.py:44
  8.7 117.1 %all-gather.11.cloned.1.call-start = ((), (), s32[]{:S(2)}) async-start(), calls=%async_computation.4 | async-start | bytes 5242880 | tf_op jit(solution)/shard_map/all_gather | solution.py:53
  27.0 179.5 %all-gather.7.cloned.1.call-start = ((), (), s32[]{:S(2)}) async-start(), calls=%async_computation.2 | async-start | bytes 5242880 | tf_op jit(solution)/shard_map/all_gather | solution.py:54
  45.3 291.3 %reduce-scatter.2.cloned.1.call-start = ((), (), s32[]{:S(2)}) async-start(), calls=%async_computation.5 | async-start | bytes 5242880 | tf_op jit(solution)/shard_map/reduce_scatter | solution.py:72
  232.1 14.9 %copy-start.2 = (f32[256,2048]{1,0:T(8,128)S(1)}, f32[256,2048]{1,0:T(8,128)}, u32[]{:S(2)}) copy-start(f32[256,2048]{1,0:T(8,128)} %fusion.16) | copy-start | bytes 6291460
  343.0 8.7 %collective-permute-start = (f32[1024,128]{1,0:T(8,128)S(1)}, f32[1024,128]{1,0:T(8,128)S(1)}, u32[]{:S(2)}, u32[]{:S(2)}) collective-permute-start(f32[1024,128]{1,0:T(8,128)S(1)} %add.250), channel_id=1, source_target_pairs={{4,0},{8,4},{12,8},{0,12},{5,1},{9,5},{13,9},{1,13},{6,2},{10,6},{... | collective-permute-start | bytes 1572872 | tf_op jit(solution)/shard_map/while/body/eval_jaxpr/ppermute | solution.py:16
  343.9 7.8 %collective-permute-start.1 = (f32[2,128]{1,0:T(2,128)S(1)}, f32[2,128]{1,0:T(2,128)S(1)}, u32[]{:S(2)}, u32[]{:S(2)}) collective-permute-start(f32[2,128]{1,0:T(2,128)S(1)} %convolution_add_fusion.3), channel_id=1, source_target_pairs={{4,0},{8,4},{12,8},{0,12},{5,1},{9,5},{13,9},{1,13},{6,2},{10,6},{... | collective-permute-start | bytes 3080 | tf_op jit(solution)/shard_map/while/body/eval_jaxpr/ppermute | solution.py:16
  353.9 8.7 %collective-permute-start = (f32[1024,128]{1,0:T(8,128)S(1)}, f32[1024,128]{1,0:T(8,128)S(1)}, u32[]{:S(2)}, u32[]{:S(2)}) collective-permute-start(f32[1024,128]{1,0:T(8,128)S(1)} %add.250), channel_id=1, source_target_pairs={{4,0},{8,4},{12,8},{0,12},{5,1},{9,5},{13,9},{1,13},{6,2},{10,6},{... | collective-permute-start | bytes 1572872 | tf_op jit(solution)/shard_map/while/body/eval_jaxpr/ppermute | solution.py:16
  354.2 8.4 %collective-permute-start.1 = (f32[2,128]{1,0:T(2,128)S(1)}, f32[2,128]{1,0:T(2,128)S(1)}, u32[]{:S(2)}, u32[]{:S(2)}) collective-permute-start(f32[2,128]{1,0:T(2,128)S(1)} %convolution_add_fusion.3), channel_id=1, source_target_pairs={{4,0},{8,4},{12,8},{0,12},{5,1},{9,5},{13,9},{1,13},{6,2},{10,6},{... | collective-permute-start | bytes 3080 | tf_op jit(solution)/shard_map/while/body/eval_jaxpr/ppermute | solution.py:16
  364.7 8.7 %collective-permute-start = (f32[1024,128]{1,0:T(8,128)S(1)}, f32[1024,128]{1,0:T(8,128)S(1)}, u32[]{:S(2)}, u32[]{:S(2)}) collective-permute-start(f32[1024,128]{1,0:T(8,128)S(1)} %add.250), channel_id=1, source_target_pairs={{4,0},{8,4},{12,8},{0,12},{5,1},{9,5},{13,9},{1,13},{6,2},{10,6},{... | collective-permute-start | bytes 1572872 | tf_op jit(solution)/shard_map/while/body/eval_jaxpr/ppermute | solution.py:16
  365.1 8.4 %collective-permute-start.1 = (f32[2,128]{1,0:T(2,128)S(1)}, f32[2,128]{1,0:T(2,128)S(1)}, u32[]{:S(2)}, u32[]{:S(2)}) collective-permute-start(f32[2,128]{1,0:T(2,128)S(1)} %convolution_add_fusion.3), channel_id=1, source_target_pairs={{4,0},{8,4},{12,8},{0,12},{5,1},{9,5},{13,9},{1,13},{6,2},{10,6},{... | collective-permute-start | bytes 3080 | tf_op jit(solution)/shard_map/while/body/eval_jaxpr/ppermute | solution.py:16
Sparse Core Ops, SparseCore 0:
  9.6 17.3 all-gather.8
  28.5 16.7 all-gather.4
  46.9 78.8 all-gather.10
  127.1 79.3 all-gather.6
  258.7 77.8 reduce-scatter.1
where the time goes:
time: 383 us; the launch traced here: 382 us
  waiting for transfers between devices  256 us (67%)
  matrix products  75.9 us (20%)
  local copies, waits for them, and re-layouts  16.3 us (4%)
  blocking collectives  15.2 us (4%)
  between operations  13.9 us (4%)
    all_gather x1, waiting for transfers between devices, local(): lax.all_gather(x_home, 'hid', axis=1, tiled=True)  72.8 us
    reduce_scatter x1, waiting for transfers between devices, local(): lax.psum_scatter(first + lax.dot_general(three_rows, d_pre_up, CONTRACT_L...  68.3 us
    all_gather x1, waiting for transfers between devices, local(): lax.all_gather(dy_home, 'hid', axis=1, tiled=True)  53.9 us
    ppermute x6, waiting for transfers between devices, passed_along(): return lax.ppermute(block, axis, route)  23.1 us
    dot_general x1, matrix products, local(): lax.dot_general(dy_piece, w_two, CONTRACT_LAST, preferred_element_type=jn...  19 us
    all_gather x1, waiting for transfers between devices, local(): lax.all_gather(grad_out, 'exp', axis=0, tiled=True)  18.2 us
    all_gather x1, waiting for transfers between devices, local(): lax.all_gather(tokens, 'exp', axis=0, tiled=True)  18.2 us
    dot_general x1, matrix products, local(): lax.dot_general(one_rows, d_pre_gate, CONTRACT_LAST, preferred_element_ty...  14.9 us
  transfers between devices with their start and end apart: 11, of which 8 were waited for; matrix products, arithmetic and copies ran while one was open for 8% of the time, Pallas kernels for 0%

commit v1 on v0

v1 whole, which is shorter than its diff:
```python
import functools
import jax
import jax.numpy as jnp
from jax import lax
from jax.experimental import pallas as pl
from jax.experimental.pallas import tpu as pltpu
from jax.sharding import PartitionSpec as P

BLOCK = 128


HIGHEST = lax.Precision.HIGHEST
CONTRACT_LAST = (((1,), (1,)), ((), ()))
MESH = pl.DeviceIdType.MESH
TILE = 512


def passed_along(block, axis, distance):
    devices = range(lax.axis_size(axis))
    route = [((i - distance) % len(devices), i) for i in devices]
    return lax.ppermute(block, axis, route)


def routing(block_experts, own_index):
    blocks_all = block_experts.shape[0]
    capacity = blocks_all // 2
    matched = block_experts == own_index
    chosen = jnp.any(matched, axis=1)
    slot_of = matched[:, 1].astype(jnp.int32)
    position = jnp.cumsum(chosen.astype(jnp.int32)) - 1
    placed = (position[None, :] == jnp.arange(capacity, dtype=jnp.int32)[:, None]) & chosen[None, :]
    placed_int = placed.astype(jnp.int32)
    list_block = jnp.sum(placed_int * jnp.arange(blocks_all, dtype=jnp.int32)[None, :], axis=1)
    list_slot = jnp.sum(placed_int * slot_of[None, :], axis=1)
    live = jnp.any(placed, axis=1)
    return list_block, list_slot, live


def dispatch_kernel(nz, ne, tok, width, tok_ref, dy_ref, gate_ref, pick_ref, slot_ref, w1_ref, w3_ref, w2_ref,
                    dpg_ref, dpu_ref, score_ref,
                    xb, db, gb, w1, w3, w2, pg, pu, dh,
                    s_up, s_dn, s_x, s_c, rsem, gs, gr, wsem, lsem):
    z = lax.axis_index("hid")
    e = lax.axis_index("exp")
    mate = e + 1 - 2 * lax.rem(e, 2)
    across = lax.rem(e + 2, ne)
    bufs = (xb, db)
    hidden = w1.shape[2]

    def weights(q, slot):
        rows = pl.ds(pl.multiple_of(q * width, width), width)
        return (
            pltpu.make_async_copy(w1_ref.at[0, rows, :], w1.at[slot], wsem.at[slot, 0]),
            pltpu.make_async_copy(w3_ref.at[0, rows, :], w3.at[slot], wsem.at[slot, 1]),
            pltpu.make_async_copy(w2_ref.at[0, :, rows], w2.at[slot], wsem.at[slot, 2]),
        )

    def send(a, zq, eq, ssem, dev):
        return pltpu.make_async_remote_copy(
            src_ref=bufs[a].at[zq, eq], dst_ref=bufs[a].at[zq, eq],
            send_sem=ssem, recv_sem=rsem.at[a, zq, eq],
            device_id=dev, device_id_type=MESH)

    def up(a, zq):
        return send(a, zq, e, s_up.at[a, zq], {"hid": z + 1})

    def down(a, zq):
        return send(a, zq, e, s_dn.at[a, zq], {"hid": z - 1})

    def over_x(a, zq):
        return send(a, zq, e, s_x.at[a, zq], {"exp": across})

    def to_mate(a, zq, eq, k):
        return send(a, zq, eq, s_c.at[a, zq, k], {"exp": mate})

    def arrived(a, zq, eq):
        send(a, zq, eq, s_x.at[a, zq], {"exp": across}).wait_recv()

    def gate_send(eq, k, dev):
        return pltpu.make_async_remote_copy(
            src_ref=gb.at[eq], dst_ref=gb.at[eq], send_sem=gs.at[k], recv_sem=gr.at[eq],
            device_id={"exp": dev}, device_id_type=MESH)

    own = (
        pltpu.make_async_copy(tok_ref, xb.at[z, e], lsem.at[0]),
        pltpu.make_async_copy(dy_ref, db.at[z, e], lsem.at[1]),
        pltpu.make_async_copy(gate_ref, gb.at[e], lsem.at[2]),
    )
    for c in own:
        c.start()
    for c in weights(z, 1):
        c.start()

    @pl.when(z > 0)
    def _():
        for c in weights(z - 1, 0):
            c.start()

    barrier = pltpu.get_barrier_semaphore()
    pl.semaphore_signal(barrier, inc=1, device_id={"exp": mate}, device_id_type=MESH)
    pl.semaphore_signal(barrier, inc=1, device_id={"exp": across}, device_id_type=MESH)

    @pl.when(z > 0)
    def _():
        pl.semaphore_signal(barrier, inc=1, device_id={"hid": z - 1}, device_id_type=MESH)

    @pl.when(z < nz - 1)
    def _():
        pl.semaphore_signal(barrier, inc=1, device_id={"hid": z + 1}, device_id_type=MESH)

    peers = 2 + (z > 0).astype(jnp.int32) + (z < nz - 1).astype(jnp.int32)
    pl.semaphore_wait(barrier, peers)

    for c in own:
        c.wait()
    for a in range(2):
        @pl.when(z < nz - 1)
        def _():
            up(a, z).start()

        @pl.when(z > 0)
        def _():
            down(a, z).start()

        over_x(a, z).start()
        to_mate(a, z, e, 0).start()
    gate_send(e, 0, across).start()
    gate_send(e, 1, mate).start()

    pg[...] = jnp.zeros_like(pg)
    pu[...] = jnp.zeros_like(pu)
    dh[...] = jnp.zeros_like(dh)

    def pass_on(d):
        for a in range(2):
            @pl.when(z - d >= 0)
            def _():
                arrived(a, z - d, e)

                @pl.when(z < nz - 1)
                def _():
                    up(a, z - d).start()

                over_x(a, z - d).start()
                to_mate(a, z - d, e, 0).start()

            @pl.when(z + d < nz)
            def _():
                arrived(a, z + d, e)

                @pl.when(z > 0)
                def _():
                    down(a, z + d).start()

                over_x(a, z + d).start()
                to_mate(a, z + d, e, 0).start()

    def from_x(zq):
        for a in range(2):
            arrived(a, zq, across)
            to_mate(a, zq, across, 1).start()

    def compute(zq, slot):
        mate_across = lax.rem(mate + 2, ne)
        for a in range(2):
            arrived(a, zq, mate)
            arrived(a, zq, mate_across)
        for c in weights(zq, slot):
            c.wait()
        pick = pick_ref[...]
        xs = jnp.dot(pick, xb[zq].reshape(ne * tok, width), preferred_element_type=jnp.float32).astype(jnp.bfloat16)
        ds = jnp.dot(pick, db[zq].reshape(ne * tok, width), preferred_element_type=jnp.float32).astype(jnp.bfloat16)

        @pl.loop(0, hidden // TILE)
        def _(t):
            cols = pl.ds(pl.multiple_of(t * TILE, TILE), TILE)
            pg[:, cols] += jnp.dot(xs, w1[slot, :, cols], preferred_element_type=jnp.float32)
            pu[:, cols] += jnp.dot(xs, w3[slot, :, cols], preferred_element_type=jnp.float32)
            dh[:, cols] += lax.dot_general(ds, w2[slot, cols, :], CONTRACT_LAST, preferred_element_type=jnp.float32)

    @pl.loop(0, nz)
    def _(d):
        @pl.when((d > 0) & (z - d >= 0))
        def _():
            from_x(z - d)

        @pl.when(z + d < nz)
        def _():
            from_x(z + d)

        @pl.when(d < nz - 1)
        def _():
            pass_on(d + 1)

        @pl.when((d > 0) & (z - d >= 0))
        def _():
            compute(z - d, 0)

            @pl.when(z - d - 1 >= 0)
            def _():
                for c in weights(z - d - 1, 0):
                    c.start()

        @pl.when(z + d < nz)
        def _():
            compute(z + d, 1)

            @pl.when(z + d + 1 < nz)
            def _():
                for c in weights(z + d + 1, 1):
                    c.start()

    gate_send(across, 2, across).wait_recv()
    gate_send(across, 2, mate).start()
    gate_send(mate, 2, mate).wait_recv()
    gate_send(lax.rem(mate + 2, ne), 2, mate).wait_recv()
    gates = jnp.dot(pick_ref[...], gb[...].reshape(ne * tok, gb.shape[2]), preferred_element_type=jnp.float32)
    gate = jnp.sum(gates * slot_ref[...], axis=1, keepdims=True)
    score_ref[...] = jnp.zeros_like(score_ref)

    @pl.loop(0, hidden // 128)
    def _(t):
        cols = pl.ds(pl.multiple_of(t * 128, 128), 128)
        g = pg[:, cols]
        u = pu[:, cols]
        h = dh[:, cols]
        sig = 1.0 / (1.0 + jnp.exp(-g))
        act = g * sig
        score_ref[...] += act * u * h
        scaled = gate * h
        dpg_ref[:, cols] = (scaled * u * sig * (1.0 + g * (1.0 - sig))).astype(jnp.bfloat16)
        dpu_ref[:, cols] = (scaled * act).astype(jnp.bfloat16)

    @pl.loop(0, nz)
    def _(q):
        for a in range(2):
            @pl.when((q <= z) & (z < nz - 1))
            def _():
                up(a, q).wait_send()

            @pl.when((q >= z) & (z > 0))
            def _():
                down(a, q).wait_send()

            over_x(a, q).wait_send()
            to_mate(a, q, e, 0).wait_send()
            to_mate(a, q, across, 1).wait_send()
    gate_send(e, 0, across).wait_send()
    gate_send(e, 1, mate).wait_send()
    gate_send(across, 2, mate).wait_send()


def dispatched(tokens, grad_out, gates, pick, slots, w_gate, w_up, w_down):
    nz, ne = lax.axis_size("hid"), lax.axis_size("exp")
    tok, width = tokens.shape
    hidden = w_gate.shape[2]
    used = pick.shape[0]
    hbm = pl.BlockSpec(memory_space=pl.ANY)
    vmem = pl.BlockSpec(memory_space=pltpu.VMEM)
    bf16, f32 = jnp.bfloat16, jnp.float32
    dma = pltpu.SemaphoreType.DMA
    return pl.pallas_call(
        functools.partial(dispatch_kernel, nz, ne, tok, width),
        out_shape=(
            jax.ShapeDtypeStruct((used, hidden), bf16),
            jax.ShapeDtypeStruct((used, hidden), bf16),
            jax.ShapeDtypeStruct((used, 128), f32),
        ),
        in_specs=[hbm, hbm, hbm, vmem, vmem, hbm, hbm, hbm],
        out_specs=(vmem, vmem, vmem),
        scratch_shapes=[
            pltpu.VMEM((nz, ne, tok, width), bf16),
            pltpu.VMEM((nz, ne, tok, width), bf16),
            pltpu.VMEM((ne, tok, 128), bf16),
            pltpu.VMEM((2, width, hidden), bf16),
            pltpu.VMEM((2, width, hidden), bf16),
            pltpu.VMEM((2, hidden, width), bf16),
            pltpu.VMEM((used, hidden), f32),
            pltpu.VMEM((used, hidden), f32),
            pltpu.VMEM((used, hidden), f32),
            dma((2, nz)),
            dma((2, nz)),
            dma((2, nz)),
            dma((2, nz, 2)),
            dma((2, nz, ne)),
            dma((3,)),
            dma((ne,)),
            dma((2, 3)),
            dma((3,)),
        ],
        compiler_params=pltpu.CompilerParams(
            collective_id=0, has_side_effects=True, vmem_limit_bytes=56 * 1024 * 1024
        ),
        cost_estimate=pl.CostEstimate(
            flops=6 * used * hidden * width * nz,
            bytes_accessed=6 * hidden * width * nz,
            transcendentals=used * hidden,
        ),
        name="dispatch",
    )(tokens, grad_out, gates, pick, slots, w_gate, w_up, w_down)


def fast_local(tokens, grad_out, gates, block_experts, w_gate, w_up, w_down):
    n_experts = lax.axis_size("exp")
    own_index = lax.axis_index("exp")
    tok_dev, width_dev = tokens.shape
    blocks_all = block_experts.shape[0]
    per_home = tok_dev // BLOCK
    capacity = blocks_all // 2
    used_count = capacity * BLOCK
    list_block, list_slot, live = routing(block_experts, own_index)
    slot_hot = (list_slot[:, None] == jnp.arange(2, dtype=jnp.int32)[None, :]).astype(jnp.float32)
    slot_hot = slot_hot * live[:, None].astype(jnp.float32)
    row = jnp.where(live, list_block * BLOCK, -used_count * n_experts)[:, None] + jnp.arange(BLOCK, dtype=jnp.int32)[None, :]
    row = row.reshape(used_count, 1)
    pick = (row == jnp.arange(blocks_all * BLOCK, dtype=jnp.int32)[None, :]).astype(jnp.bfloat16)
    lane = jnp.arange(128, dtype=jnp.int32)[None, None, :]
    slots = ((list_slot[:, None, None] == lane) & live[:, None, None]).astype(jnp.float32)
    slots = jnp.broadcast_to(slots, (capacity, BLOCK, 128)).reshape(used_count, 128)
    gates_wide = jnp.pad(gates, ((0, 0), (0, 126)))
    d_pre_gate, d_pre_up, score_lanes = dispatched(
        tokens, grad_out, gates_wide, pick, slots, w_gate, w_up, w_down
    )
    score = lax.psum(jnp.sum(score_lanes, axis=1), "hid")
    first = lax.dot_general(w_gate[0], d_pre_gate, CONTRACT_LAST, preferred_element_type=jnp.float32)
    owned = lax.psum_scatter(
        first
        + lax.dot_general(w_up[0], d_pre_up, CONTRACT_LAST, preferred_element_type=jnp.float32),
        "hid",
        scatter_dimension=0,
        tiled=True,
    )
    return combined(owned, score, list_block, live, slot_hot, tok_dev, width_dev, capacity)


def combined(owned, score, list_block, live, slot_hot, tok_dev, width_dev, capacity):
    n_experts = lax.axis_size("exp")
    own_index = lax.axis_index("exp")
    per_home = tok_dev // BLOCK
    result_cols = owned.reshape(width_dev, capacity, BLOCK)
    score_blocks = score.reshape(capacity, BLOCK)

    def share(home):
        wanted = home * per_home + jnp.arange(per_home, dtype=jnp.int32)
        select = ((list_block[None, :] == wanted[:, None]) & live[None, :]).astype(jnp.float32)
        grad_part = jnp.einsum("bi,dir->dbr", select, result_cols, precision=HIGHEST).reshape(
            width_dev, tok_dev
        )
        gate_part = jnp.einsum(
            "bi,ik,ir->kbr", select, slot_hot, score_blocks, precision=HIGHEST
        ).reshape(2, tok_dev)
        return (grad_part, gate_part)

    zero_totals = (
        jnp.zeros((width_dev, tok_dev), jnp.float32),
        jnp.zeros((2, tok_dev), jnp.float32),
    )

    def single_turn(step, totals):
        grad_part, gate_part = share((own_index + 1 + step) % n_experts)
        return passed_along((totals[0] + grad_part, totals[1] + gate_part), "exp", -1)

    totals = lax.fori_loop(0, n_experts - 1, single_turn, zero_totals)
    grad_part, gate_part = share(own_index)
    grad_total = totals[0] + grad_part
    gate_total = totals[1] + gate_part
    return (grad_total.T.astype(jnp.bfloat16), gate_total.T)


def local(tokens, grad_out, gates, block_experts, w_gate, w_up, w_down):
    own_index = lax.axis_index("exp")
    tok_dev, width_dev = tokens.shape
    blocks_all = block_experts.shape[0]
    capacity = blocks_all // 2
    used_count = capacity * BLOCK
    list_block, list_slot, live = routing(block_experts, own_index)
    row_index = (list_block[:, None] * BLOCK + jnp.arange(BLOCK, dtype=jnp.int32)[None, :]).reshape(
        used_count
    )
    x_home, dy_home, gate_home = (
        lax.all_gather(tokens, "exp", axis=0, tiled=True),
        lax.all_gather(grad_out, "exp", axis=0, tiled=True),
        lax.all_gather(gates, "exp", axis=0, tiled=True),
    )
    gate_pick = (
        jnp.take(gate_home, row_index, axis=0).astype(jnp.float32).reshape(capacity, BLOCK, 2)
    )
    slot_hot = (list_slot[:, None] == jnp.arange(2, dtype=jnp.int32)[None, :]).astype(jnp.float32)
    slot_hot = slot_hot * live[:, None].astype(jnp.float32)
    gate_column = jnp.sum(gate_pick * slot_hot[:, None, :], axis=2).reshape(used_count)
    x_piece = jnp.take(lax.all_gather(x_home, "hid", axis=1, tiled=True), row_index, axis=0)
    dy_piece = jnp.take(lax.all_gather(dy_home, "hid", axis=1, tiled=True), row_index, axis=0)
    pre_gate = jnp.dot(x_piece, w_gate[0], preferred_element_type=jnp.float32)
    pre_up = jnp.dot(x_piece, w_up[0], preferred_element_type=jnp.float32)
    d_hidden = lax.dot_general(dy_piece, w_down[0], CONTRACT_LAST, preferred_element_type=jnp.float32)
    sigmoid_gate = jax.nn.sigmoid(pre_gate)
    activated = pre_gate * sigmoid_gate
    score_part = jnp.sum(activated * pre_up * d_hidden, axis=1)
    score = lax.psum(score_part, "hid")
    scaled = gate_column[:, None] * d_hidden
    d_pre_gate = (scaled * pre_up * sigmoid_gate * (1.0 + pre_gate * (1.0 - sigmoid_gate))).astype(
        jnp.bfloat16
    )
    d_pre_up = (scaled * activated).astype(jnp.bfloat16)
    first = lax.dot_general(w_gate[0], d_pre_gate, CONTRACT_LAST, preferred_element_type=jnp.float32)
    owned = lax.psum_scatter(
        first
        + lax.dot_general(w_up[0], d_pre_up, CONTRACT_LAST, preferred_element_type=jnp.float32),
        "hid",
        scatter_dimension=0,
        tiled=True,
    )
    return combined(owned, score, list_block, live, slot_hot, tok_dev, width_dev, capacity)


def solution(mesh):
    placed = (
        P(("grp", "exp"), "hid"),
        P(("grp", "exp"), "hid"),
        P(("grp", "exp"), None),
        P("grp", None),
        P("exp", None, "hid"),
        P("exp", None, "hid"),
        P("exp", "hid", None),
    )
    body = fast_local if mesh.shape["exp"] == 4 else local
    return jax.shard_map(
        body,
        mesh=mesh,
        in_specs=placed,
        out_specs=(P(("grp", "exp"), "hid"), P(("grp", "exp"), None)),
        check_vma=False,
    )
```

time: 383 us -> 243 us (0.63)
  waiting for transfers between devices: 256 us -> 92.7 us
  Pallas kernels: 0 us -> 69.8 us
  matrix products: 75.9 us -> 41.8 us
  local copies, waits for them, and re-layouts: 16.3 us -> 4.15 us
    all_gather x4 -> x0, waiting for transfers between devices: 163 us -> none  [the longest x1 72.8 us: local(): lax.all_gather(x_home, 'hid', axis=1, tiled=True)]
    pallas_call x0 -> x1, Pallas kernels: none -> 69.8 us  [dispatched(): pl.pallas_call(functools.partial(dispatch_kernel, nz, ne, tok, width), ou...]
    dot_general x5 -> x2, matrix products: 65.7 us -> 31.7 us  [the longest x1 19.1 us: fast_local(): lax.dot_general(w_gate[0], d_pre_gate, CONTRACT_LAST, preferred_element_t...]
    gather x3 -> x0, local copies, waits for them, and re-layouts: 14.1 us -> none  [the longest x1 6.61 us: local(): jnp.take(lax.all_gather(x_home, 'hid', axis=1, tiled=True), row_index, ax...]
    all_gather x1 -> x0, blocking collectives: 5.52 us -> none  [local(): lax.all_gather(gates, 'exp', axis=0, tiled=True)]
    psum x1, blocking collectives: 9.7 us -> 13.9 us  [fast_local(): score = lax.psum(jnp.sum(score_lanes, axis=1), 'hid')]
  transfers between devices with their start and end apart: 11 -> 7, of which waited for: 8 -> 4; matrix products, arithmetic and copies ran while one was open for 8% -> 0% of each run, Pallas kernels for 0% -> 0%
where the time goes in v1:
time: 243 us; the launch traced here: 242 us
  waiting for transfers between devices  92.7 us (38%)
  Pallas kernels  69.8 us (29%)
  matrix products  41.8 us (17%)
  between operations  14.1 us (6%)
  blocking collectives  13.9 us (6%)
  local copies, waits for them, and re-layouts  4.15 us (2%)
  other arithmetic  3.23 us (1%)
    pallas_call x1, Pallas kernels, dispatched(): pl.pallas_call(functools.partial(dispatch_kernel, nz, ne, tok, width), ou...  69.8 us
    reduce_scatter x1, waiting for transfers between devices, fast_local(): lax.psum_scatter(first + lax.dot_general(w_up[0], d_pre_up, CONTRACT_LAST...  69.6 us
    ppermute x6, waiting for transfers between devices, passed_along(): return lax.ppermute(block, axis, route)  23.1 us
    dot_general x1, matrix products, fast_local(): lax.dot_general(w_gate[0], d_pre_gate, CONTRACT_LAST, preferred_element_t...  19.1 us
    psum x1, blocking collectives, fast_local(): score = lax.psum(jnp.sum(score_lanes, axis=1), 'hid')  13.9 us
    dot_general x1, matrix products, fast_local(): lax.dot_general(w_up[0], d_pre_up, CONTRACT_LAST, preferred_element_type=...  12.6 us
    while x3, matrix products  6.3 us
  transfers between devices with their start and end apart: 7, of which 4 were waited for; matrix products, arithmetic and copies ran while one was open for 0% of the time, Pallas kernels for 0%

profile of v1, /device:TPU:11, one launch (start us, length us, event | category | flops | bytes accessed | tf_op | source)
XLA Modules:
  0.0 242.1 jit_solution(5207819609190175098)
XLA Ops:
  7.2 0.0 reduce-scatter.2.cloned.1.call-start
  7.2 0.7 fusion.41
  7.9 0.2 reduce-window.8
  8.1 0.1 fusion.40
  8.2 0.1 select_reduce_fusion
  8.4 0.1 add_bitcast_fusion
  8.5 0.8 fusion.26.pick_ref
  9.3 0.1 and_convert_fusion
  9.4 0.8 copy.12
  10.2 0.6 pad.4.gate_ref
  10.8 0.6 broadcast_in_dim.17
  11.4 69.8 %dispatch.1 = (bf16[256,2048]{1,0:T(8,128)(2,1)}, bf16[256,2048]{1,0:T(8,128)(2,1)}, f32[256,128]{1,0:T(8,128)}) custom-call(bf16[128,1024]{1,0:T(8,128)(2,1)} %tok_ref.1, bf16[128,1024]{1,0:T(8,128)(2,1)} %dy_ref.1, bf16[128,128]{1,0:T(8,128)(2,1)} %pad.4.gate_ref, bf16[256,512]{1,0:T(8,128)(2,1)} %fusion.26.pick_ref, f32[256,128]{1,0:T(8,128)} %bitcast.62, ...), custom_call_target="tpu_custom_call" | custom-call | flops 12884901888 | bytes 50331648 | tf_op jit(solution)/shard_map/dispatch/pallas_call | solution.py:262
  81.2 0.0 copy-start.1
  81.2 12.6 %fusion.14 = f32[256,4096]{1,0:T(8,128)} fusion(bf16[256,2048]{1,0:T(8,128)(2,1)} %get-tuple-element.230, bf16[1,4096,2048]{2,1,0:T(8,128)(2,1)} %w3_ref.1), kind=kOutput, calls=%fused_computation.15 | convolution fusion | flops 4294967296 | bytes 22020096 | tf_op jit(solution)/shard_map/dot_general | solution.py:328
  93.8 19.1 %fusion.21 = f32[4096,256]{0,1:T(8,128)} fusion(f32[256,4096]{1,0:T(8,128)} %fusion.14, bf16[256,2048]{1,0:T(8,128)(2,1)S(1)} %copy-done.1, bf16[1,4096,2048]{2,1,0:T(8,128)(2,1)} %w1_ref.1), kind=kOutput, calls=%fused_computation.20 | convolution fusion | flops 4296015872 | bytes 26214400 | tf_op jit(solution)/shard_map/dot_general | solution.py:325
  112.9 0.0 reduce-scatter.2.cloned.1.call-update
  112.9 0.0 copy-done
  112.9 0.1 reduce_sum.29
  113.0 13.9 %psum.7 = f32[2,128]{1,0:T(2,128)S(1)} all-reduce(f32[2,128]{1,0:T(2,128)S(1)} %bitcast.63), channel_id=1, replica_groups=mesh['grp'=2,'exp'=4,'hid'=4] {'hid'}, use_global_device_ids=true, to_apply=%region_7.8 | all-reduce | flops 256 | bytes 2048 | tf_op jit(solution)/shard_map/psum | solution.py:324
  127.0 69.6 %reduce-scatter.2.cloned.1.call-done = f32[1024,256]{0,1:T(8,128)} async-done(((f32[4096,256]{0,1:T(8,128)}), f32[1024,256]{0,1:T(8,128)}) %reduce-scatter.2.cloned.1.call-update) | async-done | bytes 1048592 | tf_op jit(solution)/shard_map/reduce_scatter | solution.py:326
  196.6 1.5 copy.13
  198.1 2.2 fusion.28
  200.3 0.3 copy.15
  200.7 32.7 %while.18 = (s32[]{:T(128)}, f32[1024,128]{1,0:T(8,128)S(1)}, f32[2,128]{1,0:T(2,128)S(1)}, s32[]{:T(128)}, s32[2]{0:T(128)S(1)}, /*index=5*/pred[2]{0:T(512)(12...) while((s32[]{:T(128)}, f32[1024,128]{1,0:T(8,128)S(1)}, ...), condition=%wide.region_9.10_spmd.clone, body=%wide.region_8.9_spmd.clone.sunk | while | flops 3283236 | bytes 5250442 | solution.py:363
  200.8 2.1 fusion.57
  202.9 0.1 add.155
  203.0 0.7 collective-permute-start
  203.6 0.3 convolution_add_fusion.3
  203.9 0.1 collective-permute-start.1
  204.0 7.7 %collective-permute-done.1 = f32[2,128]{1,0:T(2,128)S(1)} collective-permute-done((f32[2,128]{1,0:T(2,128)S(1)}, f32[2,128]{1,0:T(2,128)S(1)}, u32[]{:S(2)}, u32[]{:S(2)}) %collective-permute-start.1) | collective-permute-done | bytes 1056 | tf_op jit(solution)/shard_map/while/body/eval_jaxpr/ppermute | solution.py:21
  211.7 0.0 collective-permute-done
  211.7 2.1 fusion.57
  213.8 0.1 add.155
  213.8 0.1 collective-permute-start
  213.9 0.3 convolution_add_fusion.3
  214.2 0.7 collective-permute-start.1
  214.8 7.7 %collective-permute-done.1 = f32[2,128]{1,0:T(2,128)S(1)} collective-permute-done((f32[2,128]{1,0:T(2,128)S(1)}, f32[2,128]{1,0:T(2,128)S(1)}, u32[]{:S(2)}, u32[]{:S(2)}) %collective-permute-start.1) | collective-permute-done | bytes 1056 | tf_op jit(solution)/shard_map/while/body/eval_jaxpr/ppermute | solution.py:21
  222.5 0.0 collective-permute-done
  222.5 2.1 fusion.57
  224.6 0.1 add.155
  224.7 0.1 collective-permute-start
  224.8 0.3 convolution_add_fusion.3
  225.1 0.7 collective-permute-start.1
  225.7 7.7 %collective-permute-done.1 = f32[2,128]{1,0:T(2,128)S(1)} collective-permute-done((f32[2,128]{1,0:T(2,128)S(1)}, f32[2,128]{1,0:T(2,128)S(1)}, u32[]{:S(2)}, u32[]{:S(2)}) %collective-permute-start.1) | collective-permute-done | bytes 1056 | tf_op jit(solution)/shard_map/while/body/eval_jaxpr/ppermute | solution.py:21
  233.4 0.0 collective-permute-done
  233.4 0.2 copy.14
  233.6 0.8 fusion.24
  234.5 0.8 fusion.27
  (12 shorter events, 0.1 us)
Async XLA Ops:
  7.2 189.4 %reduce-scatter.2.cloned.1.call-start = ((), (), s32[]{:S(2)}) async-start(), calls=%async_computation.1 | async-start | bytes 5242880 | tf_op jit(solution)/shard_map/reduce_scatter | solution.py:326
  81.2 12.6 %copy-start.1 = (bf16[256,2048]{1,0:T(8,128)(2,1)S(1)}, bf16[256,2048]{1,0:T(8,128)(2,1)}, u32[]{:S(2)}) copy-start(bf16[256,2048]{1,0:T(8,128)(2,1)} %get-tuple-element.229) | copy-start | bytes 3145732
  93.8 19.1 %copy-start = (f32[256,128]{1,0:T(8,128)S(1)}, f32[256,128]{1,0:T(8,128)}, u32[]{:S(2)}) copy-start(f32[256,128]{1,0:T(8,128)} %get-tuple-element.231) | copy-start | bytes 393220
  203.0 8.7 %collective-permute-start = (f32[1024,128]{1,0:T(8,128)S(1)}, f32[1024,128]{1,0:T(8,128)S(1)}, u32[]{:S(2)}, u32[]{:S(2)}) collective-permute-start(f32[1024,128]{1,0:T(8,128)S(1)} %add.155), channel_id=1, source_target_pairs={{4,0},{8,4},{12,8},{0,12},{5,1},{9,5},{13,9},{1,13},{6,2},{10,6},{... | collective-permute-start | bytes 1572872 | tf_op jit(solution)/shard_map/while/body/eval_jaxpr/ppermute | solution.py:21
  203.9 7.8 %collective-permute-start.1 = (f32[2,128]{1,0:T(2,128)S(1)}, f32[2,128]{1,0:T(2,128)S(1)}, u32[]{:S(2)}, u32[]{:S(2)}) collective-permute-start(f32[2,128]{1,0:T(2,128)S(1)} %convolution_add_fusion.3), channel_id=1, source_target_pairs={{4,0},{8,4},{12,8},{0,12},{5,1},{9,5},{13,9},{1,13},{6,2},{10,6},{... | collective-permute-start | bytes 3080 | tf_op jit(solution)/shard_map/while/body/eval_jaxpr/ppermute | solution.py:21
  213.8 8.7 %collective-permute-start = (f32[1024,128]{1,0:T(8,128)S(1)}, f32[1024,128]{1,0:T(8,128)S(1)}, u32[]{:S(2)}, u32[]{:S(2)}) collective-permute-start(f32[1024,128]{1,0:T(8,128)S(1)} %add.155), channel_id=1, source_target_pairs={{4,0},{8,4},{12,8},{0,12},{5,1},{9,5},{13,9},{1,13},{6,2},{10,6},{... | collective-permute-start | bytes 1572872 | tf_op jit(solution)/shard_map/while/body/eval_jaxpr/ppermute | solution.py:21
  214.2 8.4 %collective-permute-start.1 = (f32[2,128]{1,0:T(2,128)S(1)}, f32[2,128]{1,0:T(2,128)S(1)}, u32[]{:S(2)}, u32[]{:S(2)}) collective-permute-start(f32[2,128]{1,0:T(2,128)S(1)} %convolution_add_fusion.3), channel_id=1, source_target_pairs={{4,0},{8,4},{12,8},{0,12},{5,1},{9,5},{13,9},{1,13},{6,2},{10,6},{... | collective-permute-start | bytes 3080 | tf_op jit(solution)/shard_map/while/body/eval_jaxpr/ppermute | solution.py:21
  224.7 8.7 %collective-permute-start = (f32[1024,128]{1,0:T(8,128)S(1)}, f32[1024,128]{1,0:T(8,128)S(1)}, u32[]{:S(2)}, u32[]{:S(2)}) collective-permute-start(f32[1024,128]{1,0:T(8,128)S(1)} %add.155), channel_id=1, source_target_pairs={{4,0},{8,4},{12,8},{0,12},{5,1},{9,5},{13,9},{1,13},{6,2},{10,6},{... | collective-permute-start | bytes 1572872 | tf_op jit(solution)/shard_map/while/body/eval_jaxpr/ppermute | solution.py:21
  225.1 8.4 %collective-permute-start.1 = (f32[2,128]{1,0:T(2,128)S(1)}, f32[2,128]{1,0:T(2,128)S(1)}, u32[]{:S(2)}, u32[]{:S(2)}) collective-permute-start(f32[2,128]{1,0:T(2,128)S(1)} %convolution_add_fusion.3), channel_id=1, source_target_pairs={{4,0},{8,4},{12,8},{0,12},{5,1},{9,5},{13,9},{1,13},{6,2},{10,6},{... | collective-permute-start | bytes 3080 | tf_op jit(solution)/shard_map/while/body/eval_jaxpr/ppermute | solution.py:21
Sparse Core Ops, SparseCore 0:
  113.0 83.5 reduce-scatter.1

commit v2 on v1

--- a/solution.py
+++ b/solution.py
@@ -300,6 +300,206 @@
     )(tokens, grad_out, gates, pick, slots, w_gate, w_up, w_down)
 
 
+def combine_kernel(nz, ne, tok, width, dpg_ref, dpu_ref, scat_ref, sd_ref, w1_ref, w3_ref, out_ref, gate_ref,
+                   dense, cr, xs, xr, zs, zr, acc, w1, w3, scr, sxs, sxr, szs, szr,
+                   css, crs, xss, xrs, zss, zrs, gcs, gcr, gxs, gxr, gzs, gzr, wsem):
+    z = lax.axis_index("hid")
+    e = lax.axis_index("exp")
+    core = lax.rem(e, 2)
+    mate = e + 1 - 2 * core
+    mate_core = 1 - core
+    across = lax.rem(e + 2, ne)
+    x = e // 2
+    far = 1 - x
+
+    def weights(k, slot):
+        q = lax.rem(z + 1 + k, nz)
+        rows = pl.ds(pl.multiple_of(q * width, width), width)
+        return (
+            pltpu.make_async_copy(w1_ref.at[0, rows, :], w1.at[slot], wsem.at[slot, 0]),
+            pltpu.make_async_copy(w3_ref.at[0, rows, :], w3.at[slot], wsem.at[slot, 1]),
+        )
+
+    def remote(src, dst, ssem, rsem, dev):
+        return pltpu.make_async_remote_copy(
+            src_ref=src, dst_ref=dst, send_sem=ssem, recv_sem=rsem, device_id=dev, device_id_type=MESH)
+
+    def core_send(k, j):
+        return remote(dense.at[k, mate_core + 2 * j], cr.at[k, j], css.at[k, j], crs.at[k, j], {"exp": mate})
+
+    def x_send(k):
+        return remote(xs.at[k], xr.at[k], xss.at[k], xrs.at[k], {"exp": across})
+
+    def z_send(k):
+        return remote(zs.at[k], zr.at[z], zss.at[k], zrs.at[z], {"hid": lax.rem(z + 1 + k, nz)})
+
+    def gate_core(j):
+        return remote(sd_ref.at[mate_core + 2 * j], scr.at[j], gcs.at[j], gcr.at[j], {"exp": mate})
+
+    def gate_x():
+        return remote(sxs, sxr, gxs.at[0], gxr.at[0], {"exp": across})
+
+    def gate_z(k):
+        return remote(szs, szr.at[z], gzs.at[k], gzr.at[z], {"hid": lax.rem(z + 1 + k, nz)})
+
+    for k in range(2):
+        for c in weights(k, k):
+            c.start()
+
+    barrier = pltpu.get_barrier_semaphore()
+    pl.semaphore_signal(barrier, inc=1, device_id={"exp": mate}, device_id_type=MESH)
+    pl.semaphore_signal(barrier, inc=1, device_id={"exp": across}, device_id_type=MESH)
+    for k in range(nz - 1):
+        pl.semaphore_signal(barrier, inc=1, device_id={"hid": lax.rem(z + 1 + k, nz)}, device_id_type=MESH)
+    pl.semaphore_wait(barrier, nz + 1)
+
+    for j in range(2):
+        gate_core(j).start()
+
+    def multiply(k):
+        slot = lax.rem(k, 2)
+        for c in weights(k, slot):
+            c.wait()
+
+        @pl.loop(0, width // 256)
+        def _(t):
+            rows = pl.ds(pl.multiple_of(t * 256, 256), 256)
+            part = lax.dot_general(dpg_ref[...], w1[slot, rows, :], CONTRACT_LAST, preferred_element_type=jnp.float32)
+            part += lax.dot_general(dpu_ref[...], w3[slot, rows, :], CONTRACT_LAST, preferred_element_type=jnp.float32)
+            spread = jnp.dot(scat_ref[...], part.astype(jnp.bfloat16), preferred_element_type=jnp.float32)
+            dense[k, :, :, rows] = spread.astype(jnp.bfloat16).reshape(ne, tok, 256)
+
+        for j in range(2):
+            core_send(k, j).start()
+
+        @pl.when(k + 2 < nz)
+        def _():
+            for c in weights(k + 2, slot):
+                c.start()
+
+    def to_x(k):
+        for j in range(2):
+            core_send(k, j).wait_recv()
+        both = dense[k, core + 2 * far].astype(jnp.float32) + cr[k, far].astype(jnp.float32)
+        xs[k] = both.astype(jnp.bfloat16)
+        x_send(k).start()
+
+    def total(k):
+        x_send(k).wait_recv()
+        return (
+            dense[k, e].astype(jnp.float32) + cr[k, x].astype(jnp.float32) + xr[k].astype(jnp.float32)
+        )
+
+    def to_z(k):
+        zs[k] = total(k).astype(jnp.bfloat16)
+        z_send(k).start()
+
+    @pl.loop(0, nz)
+    def _(k):
+        multiply(k)
+        to_x(k)
+
+        @pl.when(k == 0)
+        def _():
+            for j in range(2):
+                gate_core(j).wait_recv()
+            sxs[...] = sd_ref[core + 2 * far] + scr[far]
+            gate_x().start()
+
+        @pl.when(k == 1)
+        def _():
+            gate_x().wait_recv()
+            own_sum = sd_ref[e] + scr[x] + sxr[...]
+            szs[...] = own_sum
+            szr[z] = own_sum
+            for i in range(nz - 1):
+                gate_z(i).start()
+
+        @pl.when(k >= 2)
+        def _():
+            to_z(k - 2)
+
+    to_z(nz - 2)
+    acc[...] = total(nz - 1)
+    for k in range(nz - 1):
+        source = lax.rem(z + 1 + k, nz)
+        remote(zs.at[k], zr.at[source], zss.at[k], zrs.at[source], {"hid": source}).wait_recv()
+        acc[...] += zr[source].astype(jnp.float32)
+        remote(szs, szr.at[source], gzs.at[k], gzr.at[source], {"hid": source}).wait_recv()
+    out_ref[...] = acc[...].astype(jnp.bfloat16)
+    gate_total = szr[0]
+    for q in range(1, nz):
+        gate_total += szr[q]
+    gate_ref[...] = gate_total
+
+    for j in range(2):
+        gate_core(j).wait_send()
+    gate_x().wait_send()
+    for k in range(nz):
+        for j in range(2):
+            core_send(k, j).wait_send()
+        x_send(k).wait_send()
+        if k < nz - 1:
+            z_send(k).wait_send()
+            gate_z(k).wait_send()
+
+
+def returned(d_pre_gate, d_pre_up, scatter, score_dense, w_gate, w_up, tok, width):
+    nz, ne = lax.axis_size("hid"), lax.axis_size("exp")
+    used, hidden = d_pre_gate.shape
+    hbm = pl.BlockSpec(memory_space=pl.ANY)
+    vmem = pl.BlockSpec(memory_space=pltpu.VMEM)
+    bf16, f32 = jnp.bfloat16, jnp.float32
+    dma = pltpu.SemaphoreType.DMA
+    return pl.pallas_call(
+        functools.partial(combine_kernel, nz, ne, tok, width),
+        out_shape=(
+            jax.ShapeDtypeStruct((tok, width), bf16),
+            jax.ShapeDtypeStruct((8, tok), f32),
+        ),
+        in_specs=[vmem, vmem, vmem, vmem, hbm, hbm],
+        out_specs=(vmem, vmem),
+        scratch_shapes=[
+            pltpu.VMEM((nz, ne, tok, width), bf16),
+            pltpu.VMEM((nz, 2, tok, width), bf16),
+            pltpu.VMEM((nz, tok, width), bf16),
+            pltpu.VMEM((nz, tok, width), bf16),
+            pltpu.VMEM((nz, tok, width), bf16),
+            pltpu.VMEM((nz, tok, width), bf16),
+            pltpu.VMEM((tok, width), f32),
+            pltpu.VMEM((2, width, hidden), bf16),
+            pltpu.VMEM((2, width, hidden), bf16),
+            pltpu.VMEM((2, 8, tok), f32),
+            pltpu.VMEM((8, tok), f32),
+            pltpu.VMEM((8, tok), f32),
+            pltpu.VMEM((8, tok), f32),
+            pltpu.VMEM((nz, 8, tok), f32),
+            dma((nz, 2)),
+            dma((nz, 2)),
+            dma((nz,)),
+            dma((nz,)),
+            dma((nz,)),
+            dma((nz,)),
+            dma((2,)),
+            dma((2,)),
+            dma((1,)),
+            dma((1,)),
+            dma((nz,)),
+            dma((nz,)),
+            dma((2, 2)),
+        ],
+        compiler_params=pltpu.CompilerParams(
+            collective_id=1, has_side_effects=True, vmem_limit_bytes=52 * 1024 * 1024
+        ),
+        cost_estimate=pl.CostEstimate(
+            flops=4 * used * hidden * width * nz,
+            bytes_accessed=4 * hidden * width * nz,
+            transcendentals=0,
+        ),
+        name="combine",
+    )(d_pre_gate, d_pre_up, scatter, score_dense, w_gate, w_up)
+
+
 def fast_local(tokens, grad_out, gates, block_experts, w_gate, w_up, w_down):
     n_experts = lax.axis_size("exp")
     own_index = lax.axis_index("exp")
@@ -321,16 +521,15 @@
     d_pre_gate, d_pre_up, score_lanes = dispatched(
         tokens, grad_out, gates_wide, pick, slots, w_gate, w_up, w_down
     )
-    score = lax.psum(jnp.sum(score_lanes, axis=1), "hid")
-    first = lax.dot_general(w_gate[0], d_pre_gate, CONTRACT_LAST, preferred_element_type=jnp.float32)
-    owned = lax.psum_scatter(
-        first
-        + lax.dot_general(w_up[0], d_pre_up, CONTRACT_LAST, preferred_element_type=jnp.float32),
-        "hid",
-        scatter_dimension=0,
-        tiled=True,
-    )
-    return combined(owned, score, list_block, live, slot_hot, tok_dev, width_dev, capacity)
+    score = jnp.sum(score_lanes, axis=1).reshape(capacity, BLOCK)
+    homes = jnp.arange(blocks_all, dtype=jnp.int32)
+    goes = (list_block[:, None] == homes[None, :]).astype(jnp.float32)[:, :, None] * slot_hot[:, None, :]
+    goes = jnp.pad(goes, ((0, 0), (0, 0), (0, 6)))
+    score_dense = jnp.sum(goes[:, :, :, None] * score[:, None, None, :], axis=0)
+    grad, gate_rows = returned(
+        d_pre_gate, d_pre_up, pick.T, score_dense, w_gate, w_up, tok_dev, width_dev
+    )
+    return grad, gate_rows[:2].T
 
 
 def combined(owned, score, list_block, live, slot_hot, tok_dev, width_dev, capacity):
@@ -423,7 +622,7 @@
         P("exp", None, "hid"),
         P("exp", "hid", None),
     )
-    body = fast_local if mesh.shape["exp"] == 4 else local
+    body = fast_local if (mesh.shape["exp"], mesh.shape["hid"]) == (4, 4) else local
     return jax.shard_map(
         body,
         mesh=mesh,

time: 243 us -> 136 us (0.56)
  waiting for transfers between devices: 92.7 us -> 0 us
  Pallas kernels: 69.8 us -> 127 us
  matrix products: 41.8 us -> 0 us
  blocking collectives: 13.9 us -> 0 us
  between operations: 14.1 us -> 0.69 us
    reduce_scatter x1 -> x0, waiting for transfers between devices: 69.6 us -> none  [fast_local(): lax.psum_scatter(first + lax.dot_general(w_up[0], d_pre_up, CONTRACT_LAST...]
    pallas_call x0 -> x1, Pallas kernels: none -> 56.9 us  [returned(): pl.pallas_call(functools.partial(combine_kernel, nz, ne, tok, width), out...]
    dot_general x7 -> x0, matrix products: 35.5 us -> none  [the longest x1 19.1 us: fast_local(): lax.dot_general(w_gate[0], d_pre_gate, CONTRACT_LAST, preferred_element_t...]
    ppermute x6 -> x0, waiting for transfers between devices: 23.1 us -> none  [passed_along(): return lax.ppermute(block, axis, route)]
    psum x1 -> x0, blocking collectives: 13.9 us -> none  [fast_local(): score = lax.psum(jnp.sum(score_lanes, axis=1), 'hid')]
    while x3 -> x0, matrix products: 6.3 us -> none
  transfers between devices with their start and end apart: 7 -> 0, of which waited for: 4 -> 0; matrix products, arithmetic and copies ran while one was open for 0% -> 0% of each run, Pallas kernels for 0% -> 0%
where the time goes in v2:
time: 136 us; the launch traced here: 135 us
  Pallas kernels  127 us (93%)
  local copies, waits for them, and re-layouts  4.55 us (3%)
  other arithmetic  3.53 us (3%)
    pallas_call x1, Pallas kernels, dispatched(): pl.pallas_call(functools.partial(dispatch_kernel, nz, ne, tok, width), ou...  69.8 us
    pallas_call x1, Pallas kernels, returned(): pl.pallas_call(functools.partial(combine_kernel, nz, ne, tok, width), out...  56.9 us

profile of v2, /device:TPU:11, one launch (start us, length us, event | category | flops | bytes accessed | tf_op | source)
XLA Modules:
  0.0 135.5 jit_solution(3450569714510773918)
XLA Ops:
  0.6 0.7 fusion.3
  1.3 0.2 reduce-window.8
  1.5 0.1 select_reduce_fusion
  1.7 0.1 reduce_or.19
  1.8 0.1 add_bitcast_fusion
  1.9 0.8 fusion.pick_ref
  2.7 0.1 and_convert_fusion
  2.8 0.7 broadcast_in_dim.6
  3.5 0.8 copy.10
  4.2 0.6 pad.8.gate_ref
  4.8 69.8 %dispatch.1 = (bf16[256,2048]{1,0:T(8,128)(2,1)}, bf16[256,2048]{1,0:T(8,128)(2,1)}, f32[256,128]{1,0:T(8,128)}) custom-call(bf16[128,1024]{1,0:T(8,128)(2,1)} %tok_ref.1, bf16[128,1024]{1,0:T(8,128)(2,1)} %dy_ref.1, bf16[128,128]{1,0:T(8,128)(2,1)} %pad.8.gate_ref, bf16[256,512]{1,0:T(8,128)(2,1)} %fusion.pick_ref, f32[256,128]{1,0:T(8,128)} %bitcast.12, ...), custom_call_target="tpu_custom_call" | custom-call | flops 12884901888 | bytes 50331648 | tf_op jit(solution)/shard_map/dispatch/pallas_call | solution.py:262
  74.7 1.0 reduce_sum.38
  75.7 0.1 compare_select_fusion
  75.8 0.1 compare_convert_fusion
  75.8 0.1 broadcast_multiply_fusion
  75.9 0.1 multiply_reduce_fusion.sd_ref
  76.0 0.1 fusion.1.scat_ref
  76.1 0.0 copy-start
  76.1 1.2 copy-done
  77.3 56.9 %combine.1 = (bf16[128,1024]{1,0:T(8,128)(2,1)S(1)}, f32[8,128]{1,0:T(8,128)S(1)}) custom-call(bf16[256,2048]{1,0:T(8,128)(2,1)S(1)} %copy-done, bf16[256,2048]{1,0:T(8,128)(2,1)} %get-tuple-element.8.dpu_ref, bf16[512,256]{1,0:T(8,128)(2,1)S(1)} %fusion.1.scat_ref, f32[4,8,128]{2,1,0:T(8,128)S(1)} %multiply_reduce_fusion.sd_ref, ...), custom_call_target="tpu_custom_call" | custom-call | flops 8589934592 | bytes 33554432 | tf_op jit(solution)/shard_map/combine/pallas_call | solution.py:454
  134.2 0.6 slice_bitcast_fusion
  134.8 0.7 copy.12
  (6 shorter events, 0.0 us)
Async XLA Ops:
  76.1 1.2 copy-start

commit v3 on v2

--- a/solution.py
+++ b/solution.py
@@ -155,39 +155,38 @@
                 over_x(a, z + d).start()
                 to_mate(a, z + d, e, 0).start()
 
-    def from_x(zq):
-        for a in range(2):
-            arrived(a, zq, across)
-            to_mate(a, zq, across, 1).start()
+    mate_across = lax.rem(mate + 2, ne)
+
+    def picked(a, zq):
+        arrived(a, zq, across)
+        to_mate(a, zq, across, 1).start()
+        arrived(a, zq, mate)
+        arrived(a, zq, mate_across)
+        rows = bufs[a][zq].reshape(ne * tok, width)
+        return jnp.dot(pick_ref[...], rows, preferred_element_type=jnp.float32).astype(jnp.bfloat16)
 
     def compute(zq, slot):
-        mate_across = lax.rem(mate + 2, ne)
-        for a in range(2):
-            arrived(a, zq, mate)
-            arrived(a, zq, mate_across)
-        for c in weights(zq, slot):
-            c.wait()
-        pick = pick_ref[...]
-        xs = jnp.dot(pick, xb[zq].reshape(ne * tok, width), preferred_element_type=jnp.float32).astype(jnp.bfloat16)
-        ds = jnp.dot(pick, db[zq].reshape(ne * tok, width), preferred_element_type=jnp.float32).astype(jnp.bfloat16)
+        pending = weights(zq, slot)
+        xs = picked(0, zq)
+        pending[0].wait()
+        pending[1].wait()
 
         @pl.loop(0, hidden // TILE)
         def _(t):
             cols = pl.ds(pl.multiple_of(t * TILE, TILE), TILE)
             pg[:, cols] += jnp.dot(xs, w1[slot, :, cols], preferred_element_type=jnp.float32)
             pu[:, cols] += jnp.dot(xs, w3[slot, :, cols], preferred_element_type=jnp.float32)
+
+        ds = picked(1, zq)
+        pending[2].wait()
+
+        @pl.loop(0, hidden // TILE)
+        def _(t):
+            cols = pl.ds(pl.multiple_of(t * TILE, TILE), TILE)
             dh[:, cols] += lax.dot_general(ds, w2[slot, cols, :], CONTRACT_LAST, preferred_element_type=jnp.float32)
 
     @pl.loop(0, nz)
     def _(d):
-        @pl.when((d > 0) & (z - d >= 0))
-        def _():
-            from_x(z - d)
-
-        @pl.when(z + d < nz)
-        def _():
-            from_x(z + d)
-
         @pl.when(d < nz - 1)
         def _():
             pass_on(d + 1)

time: 136 us -> 129 us (0.949)
  Pallas kernels: 127 us -> 119 us
    pallas_call x1, Pallas kernels: 56.9 us -> 51.6 us  [returned(): pl.pallas_call(functools.partial(combine_kernel, nz, ne, tok, width), out...]
    pallas_call x1, Pallas kernels: 69.8 us -> 67 us  [dispatched(): pl.pallas_call(functools.partial(dispatch_kernel, nz, ne, tok, width), ou...]
where the time goes in v3:
time: 129 us; the launch traced here: 127 us
  Pallas kernels  119 us (92%)
  local copies, waits for them, and re-layouts  4.55 us (4%)
  other arithmetic  3.53 us (3%)
    pallas_call x1, Pallas kernels, dispatched(): pl.pallas_call(functools.partial(dispatch_kernel, nz, ne, tok, width), ou...  67 us
    pallas_call x1, Pallas kernels, returned(): pl.pallas_call(functools.partial(combine_kernel, nz, ne, tok, width), out...  51.6 us
    unnamed x4, local copies, waits for them, and re-layouts  2.7 us

profile of v3, /device:TPU:11, one launch (start us, length us, event | category | flops | bytes accessed | tf_op | source)
XLA Modules:
  0.0 127.4 jit_solution(6532886443187792088)
XLA Ops:
  0.6 0.7 fusion.3
  1.3 0.2 reduce-window.8
  1.5 0.1 select_reduce_fusion
  1.7 0.1 reduce_or.19
  1.8 0.1 add_bitcast_fusion
  1.9 0.8 fusion.pick_ref
  2.7 0.1 and_convert_fusion
  2.8 0.7 broadcast_in_dim.6
  3.5 0.8 copy.10
  4.2 0.6 pad.8.gate_ref
  4.8 67.0 %dispatch.1 = (bf16[256,2048]{1,0:T(8,128)(2,1)}, bf16[256,2048]{1,0:T(8,128)(2,1)}, f32[256,128]{1,0:T(8,128)}) custom-call(bf16[128,1024]{1,0:T(8,128)(2,1)} %tok_ref.1, bf16[128,1024]{1,0:T(8,128)(2,1)} %dy_ref.1, bf16[128,128]{1,0:T(8,128)(2,1)} %pad.8.gate_ref, bf16[256,512]{1,0:T(8,128)(2,1)} %fusion.pick_ref, f32[256,128]{1,0:T(8,128)} %bitcast.12, ...), custom_call_target="tpu_custom_call" | custom-call | flops 12884901888 | bytes 50331648 | tf_op jit(solution)/shard_map/dispatch/pallas_call | solution.py:261
  71.9 1.0 reduce_sum.38
  72.9 0.1 compare_select_fusion
  73.0 0.1 compare_convert_fusion
  73.0 0.1 broadcast_multiply_fusion
  73.1 0.1 multiply_reduce_fusion.sd_ref
  73.2 0.1 fusion.1.scat_ref
  73.3 0.0 copy-start
  73.3 1.2 copy-done
  74.5 51.6 %combine.1 = (bf16[128,1024]{1,0:T(8,128)(2,1)S(1)}, f32[8,128]{1,0:T(8,128)S(1)}) custom-call(bf16[256,2048]{1,0:T(8,128)(2,1)S(1)} %copy-done, bf16[256,2048]{1,0:T(8,128)(2,1)} %get-tuple-element.8.dpu_ref, bf16[512,256]{1,0:T(8,128)(2,1)S(1)} %fusion.1.scat_ref, f32[4,8,128]{2,1,0:T(8,128)S(1)} %multiply_reduce_fusion.sd_ref, ...), custom_call_target="tpu_custom_call" | custom-call | flops 8589934592 | bytes 33554432 | tf_op jit(solution)/shard_map/combine/pallas_call | solution.py:453
  126.1 0.6 slice_bitcast_fusion
  126.7 0.7 copy.12
  (6 shorter events, 0.0 us)
Async XLA Ops:
  73.3 1.2 copy-start

commit v4 on v1

--- a/solution.py
+++ b/solution.py
@@ -36,10 +36,12 @@
     return list_block, list_slot, live
 
 
-def dispatch_kernel(nz, ne, tok, width, tok_ref, dy_ref, gate_ref, pick_ref, slot_ref, w1_ref, w3_ref, w2_ref,
-                    dpg_ref, dpu_ref, score_ref,
-                    xb, db, gb, w1, w3, w2, pg, pu, dh,
-                    s_up, s_dn, s_x, s_c, rsem, gs, gr, wsem, lsem):
+def layer_kernel(nz, ne, tok, width, tok_ref, dy_ref, gate_ref, pick_ref, slot_ref, home_ref, scat_ref,
+                 w1_ref, w3_ref, w2_ref, out_ref, grad_gate_ref,
+                 xb, db, gb, w1, w3, w2, pg, pu, dh, dpg_ref, dpu_ref, score_ref, sd_ref,
+                 dense, cr, xs, xr, zs, zr, acc, scr, sxs, sxr, szs, szr,
+                 s_up, s_dn, s_x, s_c, rsem, gs, gr, wsem, lsem,
+                 css, crs, xss, xrs, zss, zrs, gcs, gcr, gxs, gxr, gzs, gzr):
     z = lax.axis_index("hid")
     e = lax.axis_index("exp")
     mate = e + 1 - 2 * lax.rem(e, 2)
@@ -100,16 +102,9 @@
     pl.semaphore_signal(barrier, inc=1, device_id={"exp": mate}, device_id_type=MESH)
     pl.semaphore_signal(barrier, inc=1, device_id={"exp": across}, device_id_type=MESH)
 
-    @pl.when(z > 0)
-    def _():
-        pl.semaphore_signal(barrier, inc=1, device_id={"hid": z - 1}, device_id_type=MESH)
-
-    @pl.when(z < nz - 1)
-    def _():
-        pl.semaphore_signal(barrier, inc=1, device_id={"hid": z + 1}, device_id_type=MESH)
-
-    peers = 2 + (z > 0).astype(jnp.int32) + (z < nz - 1).astype(jnp.int32)
-    pl.semaphore_wait(barrier, peers)
+    for k in range(nz - 1):
+        pl.semaphore_signal(barrier, inc=1, device_id={"hid": lax.rem(z + 1 + k, nz)}, device_id_type=MESH)
+    pl.semaphore_wait(barrier, nz + 1)
 
     for c in own:
         c.wait()
@@ -155,39 +150,38 @@
                 over_x(a, z + d).start()
                 to_mate(a, z + d, e, 0).start()
 
-    def from_x(zq):
-        for a in range(2):
-            arrived(a, zq, across)
-            to_mate(a, zq, across, 1).start()
+    mate_across = lax.rem(mate + 2, ne)
+
+    def picked(a, zq):
+        arrived(a, zq, across)
+        to_mate(a, zq, across, 1).start()
+        arrived(a, zq, mate)
+        arrived(a, zq, mate_across)
+        rows = bufs[a][zq].reshape(ne * tok, width)
+        return jnp.dot(pick_ref[...], rows, preferred_element_type=jnp.float32).astype(jnp.bfloat16)
 
     def compute(zq, slot):
-        mate_across = lax.rem(mate + 2, ne)
-        for a in range(2):
-            arrived(a, zq, mate)
-            arrived(a, zq, mate_across)
-        for c in weights(zq, slot):
-            c.wait()
-        pick = pick_ref[...]
-        xs = jnp.dot(pick, xb[zq].reshape(ne * tok, width), preferred_element_type=jnp.float32).astype(jnp.bfloat16)
-        ds = jnp.dot(pick, db[zq].reshape(ne * tok, width), preferred_element_type=jnp.float32).astype(jnp.bfloat16)
+        pending = weights(zq, slot)
+        xs = picked(0, zq)
+        pending[0].wait()
+        pending[1].wait()
 
         @pl.loop(0, hidden // TILE)
         def _(t):
             cols = pl.ds(pl.multiple_of(t * TILE, TILE), TILE)
             pg[:, cols] += jnp.dot(xs, w1[slot, :, cols], preferred_element_type=jnp.float32)
             pu[:, cols] += jnp.dot(xs, w3[slot, :, cols], preferred_element_type=jnp.float32)
+
+        ds = picked(1, zq)
+        pending[2].wait()
+
+        @pl.loop(0, hidden // TILE)
+        def _(t):
+            cols = pl.ds(pl.multiple_of(t * TILE, TILE), TILE)
             dh[:, cols] += lax.dot_general(ds, w2[slot, cols, :], CONTRACT_LAST, preferred_element_type=jnp.float32)
 
     @pl.loop(0, nz)
     def _(d):
-        @pl.when((d > 0) & (z - d >= 0))
-        def _():
-            from_x(z - d)
-
-        @pl.when(z + d < nz)
-        def _():
-            from_x(z + d)
-
         @pl.when(d < nz - 1)
         def _():
             pass_on(d + 1)
@@ -209,6 +203,45 @@
             def _():
                 for c in weights(z + d + 1, 1):
                     c.start()
+
+    core = lax.rem(e, 2)
+    mate_core = 1 - core
+    x = e // 2
+    far = 1 - x
+
+    def again(k, slot):
+        q = lax.rem(z + 1 + k, nz)
+        rows = pl.ds(pl.multiple_of(q * width, width), width)
+        return (
+            pltpu.make_async_copy(w1_ref.at[0, rows, :], w1.at[slot], wsem.at[slot, 0]),
+            pltpu.make_async_copy(w3_ref.at[0, rows, :], w3.at[slot], wsem.at[slot, 1]),
+        )
+
+    def remote(src, dst, ssem, rsem, dev):
+        return pltpu.make_async_remote_copy(
+            src_ref=src, dst_ref=dst, send_sem=ssem, recv_sem=rsem, device_id=dev, device_id_type=MESH)
+
+    def core_send(k, j):
+        return remote(dense.at[k, mate_core + 2 * j], cr.at[k, j], css.at[k, j], crs.at[k, j], {"exp": mate})
+
+    def x_send(k):
+        return remote(xs.at[k], xr.at[k], xss.at[k], xrs.at[k], {"exp": across})
+
+    def z_send(k):
+        return remote(zs.at[k], zr.at[z], zss.at[k], zrs.at[z], {"hid": lax.rem(z + 1 + k, nz)})
+
+    def gate_core(j):
+        return remote(sd_ref.at[mate_core + 2 * j], scr.at[j], gcs.at[j], gcr.at[j], {"exp": mate})
+
+    def gate_x():
+        return remote(sxs, sxr, gxs.at[0], gxr.at[0], {"exp": across})
+
+    def gate_z(k):
+        return remote(szs, szr.at[z], gzs.at[k], gzr.at[z], {"hid": lax.rem(z + 1 + k, nz)})
+
+    for k in range(2):
+        for c in again(k, k):
+            c.start()
 
     gate_send(across, 2, across).wait_recv()
     gate_send(across, 2, mate).start()
@@ -231,6 +264,104 @@
         dpg_ref[:, cols] = (scaled * u * sig * (1.0 + g * (1.0 - sig))).astype(jnp.bfloat16)
         dpu_ref[:, cols] = (scaled * act).astype(jnp.bfloat16)
 
+    score = jnp.sum(score_ref[...], axis=1, keepdims=True) * slot_ref[...]
+    for home in range(ne):
+        mine = score * home_ref[:, home : home + 1]
+        placed = mine[:tok]
+        for i in range(1, mine.shape[0] // tok):
+            placed += mine[i * tok : (i + 1) * tok]
+        sd_ref[home] = placed
+
+    for j in range(2):
+        gate_core(j).start()
+
+    def multiply(k):
+        slot = lax.rem(k, 2)
+        for c in again(k, slot):
+            c.wait()
+
+        @pl.loop(0, width // 256)
+        def _(t):
+            rows = pl.ds(pl.multiple_of(t * 256, 256), 256)
+            part = lax.dot_general(dpg_ref[...], w1[slot, rows, :], CONTRACT_LAST, preferred_element_type=jnp.float32)
+            part += lax.dot_general(dpu_ref[...], w3[slot, rows, :], CONTRACT_LAST, preferred_element_type=jnp.float32)
+            spread = jnp.dot(scat_ref[...], part.astype(jnp.bfloat16), preferred_element_type=jnp.float32)
+            dense[k, :, :, rows] = spread.astype(jnp.bfloat16).reshape(ne, tok, 256)
+
+        for j in range(2):
+            core_send(k, j).start()
+
+        @pl.when(k + 2 < nz)
+        def _():
+            for c in again(k + 2, slot):
+                c.start()
+
+    def to_x(k):
+        for j in range(2):
+            core_send(k, j).wait_recv()
+        both = dense[k, core + 2 * far].astype(jnp.float32) + cr[k, far].astype(jnp.float32)
+        xs[k] = both.astype(jnp.bfloat16)
+        x_send(k).start()
+
+    def total(k):
+        x_send(k).wait_recv()
+        return (
+            dense[k, e].astype(jnp.float32) + cr[k, x].astype(jnp.float32) + xr[k].astype(jnp.float32)
+        )
+
+    def to_z(k):
+        zs[k] = total(k).astype(jnp.bfloat16)
+        z_send(k).start()
+
+    @pl.loop(0, nz)
+    def _(k):
+        multiply(k)
+        to_x(k)
+
+        @pl.when(k == 0)
+        def _():
+            for j in range(2):
+                gate_core(j).wait_recv()
+            sxs[...] = sd_ref[core + 2 * far] + scr[far]
+            gate_x().start()
+
+        @pl.when(k == 1)
+        def _():
+            gate_x().wait_recv()
+            own_sum = sd_ref[e] + scr[x] + sxr[...]
+            szs[...] = own_sum
+            szr[z] = own_sum
+            for i in range(nz - 1):
+                gate_z(i).start()
+
+        @pl.when(k >= 2)
+        def _():
+            to_z(k - 2)
+
+    to_z(nz - 2)
+    acc[...] = total(nz - 1)
+    for k in range(nz - 1):
+        source = lax.rem(z + 1 + k, nz)
+        remote(zs.at[k], zr.at[source], zss.at[k], zrs.at[source], {"hid": source}).wait_recv()
+        acc[...] += zr[source].astype(jnp.float32)
+        remote(szs, szr.at[source], gzs.at[k], gzr.at[source], {"hid": source}).wait_recv()
+    out_ref[...] = acc[...].astype(jnp.bfloat16)
+    gate_total = szr[0]
+    for q in range(1, nz):
+        gate_total += szr[q]
+    grad_gate_ref[...] = gate_total
+
+    for j in range(2):
+        gate_core(j).wait_send()
+    gate_x().wait_send()
+    for k in range(nz):
+        for j in range(2):
+            core_send(k, j).wait_send()
+        x_send(k).wait_send()
+        if k < nz - 1:
+            z_send(k).wait_send()
+            gate_z(k).wait_send()
+
     @pl.loop(0, nz)
     def _(q):
         for a in range(2):
@@ -250,7 +381,7 @@
     gate_send(across, 2, mate).wait_send()
 
 
-def dispatched(tokens, grad_out, gates, pick, slots, w_gate, w_up, w_down):
+def layer(tokens, grad_out, gates, pick, slots, homes, w_gate, w_up, w_down):
     nz, ne = lax.axis_size("hid"), lax.axis_size("exp")
     tok, width = tokens.shape
     hidden = w_gate.shape[2]
@@ -260,14 +391,13 @@
     bf16, f32 = jnp.bfloat16, jnp.float32
     dma = pltpu.SemaphoreType.DMA
     return pl.pallas_call(
-        functools.partial(dispatch_kernel, nz, ne, tok, width),
+        functools.partial(layer_kernel, nz, ne, tok, width),
         out_shape=(
-            jax.ShapeDtypeStruct((used, hidden), bf16),
-            jax.ShapeDtypeStruct((used, hidden), bf16),
-            jax.ShapeDtypeStruct((used, 128), f32),
+            jax.ShapeDtypeStruct((tok, width), bf16),
+            jax.ShapeDtypeStruct((tok, 128), f32),
         ),
-        in_specs=[hbm, hbm, hbm, vmem, vmem, hbm, hbm, hbm],
-        out_specs=(vmem, vmem, vmem),
+        in_specs=[hbm, hbm, hbm, vmem, vmem, vmem, vmem, hbm, hbm, hbm],
+        out_specs=(vmem, vmem),
         scratch_shapes=[
             pltpu.VMEM((nz, ne, tok, width), bf16),
             pltpu.VMEM((nz, ne, tok, width), bf16),
@@ -278,6 +408,22 @@
             pltpu.VMEM((used, hidden), f32),
             pltpu.VMEM((used, hidden), f32),
             pltpu.VMEM((used, hidden), f32),
+            pltpu.VMEM((used, hidden), bf16),
+            pltpu.VMEM((used, hidden), bf16),
+            pltpu.VMEM((used, 128), f32),
+            pltpu.VMEM((ne, tok, 128), f32),
+            pltpu.VMEM((nz, ne, tok, width), bf16),
+            pltpu.VMEM((nz, 2, tok, width), bf16),
+            pltpu.VMEM((nz, tok, width), bf16),
+            pltpu.VMEM((nz, tok, width), bf16),
+            pltpu.VMEM((nz, tok, width), bf16),
+            pltpu.VMEM((nz, tok, width), bf16),
+            pltpu.VMEM((tok, width), f32),
+            pltpu.VMEM((2, tok, 128), f32),
+            pltpu.VMEM((tok, 128), f32),
+            pltpu.VMEM((tok, 128), f32),
+            pltpu.VMEM((tok, 128), f32),
+            pltpu.VMEM((nz, tok, 128), f32),
             dma((2, nz)),
             dma((2, nz)),
             dma((2, nz)),
@@ -287,17 +433,24 @@
             dma((ne,)),
             dma((2, 3)),
             dma((3,)),
+            dma((nz, 2)),
+            dma((nz, 2)),
+            dma((nz,)),
+            dma((nz,)),
+            dma((nz,)),
+            dma((nz,)),
+            dma((2,)),
+            dma((2,)),
+            dma((1,)),
+            dma((1,)),
+            dma((nz,)),
+            dma((nz,)),
         ],
         compiler_params=pltpu.CompilerParams(
-            collective_id=0, has_side_effects=True, vmem_limit_bytes=56 * 1024 * 1024
+            collective_id=0, has_side_effects=True, vmem_limit_bytes=60 * 1024 * 1024
         ),
-        cost_estimate=pl.CostEstimate(
-            flops=6 * used * hidden * width * nz,
-            bytes_accessed=6 * hidden * width * nz,
-            transcendentals=used * hidden,
-        ),
-        name="dispatch",
-    )(tokens, grad_out, gates, pick, slots, w_gate, w_up, w_down)
+        name="layer",
+    )(tokens, grad_out, gates, pick, slots, homes, pick.T, w_gate, w_up, w_down)
 
 
 def fast_local(tokens, grad_out, gates, block_experts, w_gate, w_up, w_down):
@@ -318,19 +471,10 @@
     slots = ((list_slot[:, None, None] == lane) & live[:, None, None]).astype(jnp.float32)
     slots = jnp.broadcast_to(slots, (capacity, BLOCK, 128)).reshape(used_count, 128)
     gates_wide = jnp.pad(gates, ((0, 0), (0, 126)))
-    d_pre_gate, d_pre_up, score_lanes = dispatched(
-        tokens, grad_out, gates_wide, pick, slots, w_gate, w_up, w_down
-    )
-    score = lax.psum(jnp.sum(score_lanes, axis=1), "hid")
-    first = lax.dot_general(w_gate[0], d_pre_gate, CONTRACT_LAST, preferred_element_type=jnp.float32)
-    owned = lax.psum_scatter(
-        first
-        + lax.dot_general(w_up[0], d_pre_up, CONTRACT_LAST, preferred_element_type=jnp.float32),
-        "hid",
-        scatter_dimension=0,
-        tiled=True,
-    )
-    return combined(owned, score, list_block, live, slot_hot, tok_dev, width_dev, capacity)
+    homes = ((list_block[:, None, None] == lane) & live[:, None, None]).astype(jnp.float32)
+    homes = jnp.broadcast_to(homes, (capacity, BLOCK, 128)).reshape(used_count, 128)
+    grad, gate_lanes = layer(tokens, grad_out, gates_wide, pick, slots, homes, w_gate, w_up, w_down)
+    return grad, gate_lanes[:, :2]
 
 
 def combined(owned, score, list_block, live, slot_hot, tok_dev, width_dev, capacity):
@@ -423,7 +567,7 @@
         P("exp", None, "hid"),
         P("exp", "hid", None),
     )
-    body = fast_local if mesh.shape["exp"] == 4 else local
+    body = fast_local if (mesh.shape["exp"], mesh.shape["hid"]) == (4, 4) else local
     return jax.shard_map(
         body,
         mesh=mesh,

time: 243 us -> 126 us (0.52)
  waiting for transfers between devices: 92.7 us -> 0 us
  Pallas kernels: 69.8 us -> 115 us
  matrix products: 41.8 us -> 0 us
  blocking collectives: 13.9 us -> 0 us
  between operations: 14.1 us -> 0.66 us
    reduce_scatter x1 -> x0, waiting for transfers between devices: 69.6 us -> none  [fast_local(): lax.psum_scatter(first + lax.dot_general(w_up[0], d_pre_up, CONTRACT_LAST...]
    pallas_call x1, Pallas kernels: 69.8 us -> 115 us  [layer(): pl.pallas_call(functools.partial(layer_kernel, nz, ne, tok, width), out_s...]
    dot_general x7 -> x0, matrix products: 35.5 us -> none  [the longest x1 19.1 us: fast_local(): lax.dot_general(w_gate[0], d_pre_gate, CONTRACT_LAST, preferred_element_t...]
    ppermute x6 -> x0, waiting for transfers between devices: 23.1 us -> none  [passed_along(): return lax.ppermute(block, axis, route)]
    psum x1 -> x0, blocking collectives: 13.9 us -> none  [fast_local(): score = lax.psum(jnp.sum(score_lanes, axis=1), 'hid')]
    while x3 -> x0, matrix products: 6.3 us -> none
  transfers between devices with their start and end apart: 7 -> 0, of which waited for: 4 -> 0; matrix products, arithmetic and copies ran while one was open for 0% -> 0% of each run, Pallas kernels for 0% -> 0%
where the time goes in v4:
time: 126 us; the launch traced here: 125 us
  Pallas kernels  115 us (91%)
  local copies, waits for them, and re-layouts  5.85 us (5%)
  other arithmetic  2.89 us (2%)
    pallas_call x1, Pallas kernels, layer(): pl.pallas_call(functools.partial(layer_kernel, nz, ne, tok, width), out_s...  115 us
    unnamed x3, local copies, waits for them, and re-layouts  3.93 us

profile of v4, /device:TPU:11, one launch (start us, length us, event | category | flops | bytes accessed | tf_op | source)
XLA Modules:
  0.0 124.7 jit_solution(9850422649398071382)
XLA Ops:
  0.6 0.7 fusion.3
  1.4 0.2 reduce-window.8
  1.5 0.1 select_reduce_fusion
  1.7 0.1 reduce_or.19
  1.8 0.1 add_bitcast_fusion
  1.9 0.1 and_convert_fusion
  2.0 0.8 copy.11
  2.8 0.6 pad.4.gate_ref
  3.4 0.6 broadcast_in_dim.10
  4.0 0.7 broadcast_in_dim.9
  4.7 0.8 fusion.1.scat_ref
  5.4 0.8 fusion.pick_ref
  6.3 115.3 %layer.1 = (bf16[128,1024]{1,0:T(8,128)(2,1)}, f32[128,128]{1,0:T(8,128)}) custom-call(bf16[128,1024]{1,0:T(8,128)(2,1)} %tok_ref.1, bf16[128,1024]{1,0:T(8,128)(2,1)} %dy_ref.1, bf16[128,128]{1,0:T(8,128)(2,1)} %pad.4.gate_ref, bf16[256,512]{1,0:T(8,128)(2,1)} %fusion.pick_ref, f32[256,128]{1,0:T(8,128)} %bitcast.12, f32[256,128]{1,0:T(8,128)} %bitcast.11, ...), custom_call_target="tpu_custom_call" | custom-call | tf_op jit(solution)/shard_map/layer/pallas_call | solution.py:393
  121.5 1.5 %copy.12 = f32[128,2]{0,1:T(2,128)} copy(f32[128,2]{1,0:T(8,128)} %bitcast.13) | data formatting | bytes 2048
  123.0 1.7 %copy.14 = bf16[128,1024]{1,0:T(8,128)(2,1)} copy(bf16[128,1024]{1,0:T(8,128)(2,1)} %get-tuple-element.19) | data formatting | bytes 524288
  (4 shorter events, 0.0 us)
